TPU v7x, 256 devices: a whole 4x4x8 slice. The times are simulated.
256 devices in a mesh: row: 16 (over y, x_lo, core), col: 16 (over x_hi, z).
Axes of the slice: x: 4 (x_hi: 2, x_lo: 2; x = x_hi * 2 + x_lo), y: 4, z: 8, core: 2. Of those that a mesh axis runs over, the one named last changes fastest.
Arguments:
- grads: bfloat16 [8192, 8192], P('row'), may hold values from -0.0625 to 0.0625
- seeds: int32 [8192], replicated, may hold values from 0 to 12
- bank: bfloat16 [256, 8192], P('row'), may hold values from -6 to 6
- query_ids: int32 [128], replicated, may hold values from 0 to 255, as said below
Outputs:
- solution: float32 [8192, 128], P('row')
- residual: float32 [8192, 128], P('row')
Inputs may be any that keep to these rules, and one draw needn't show every extreme that they name: `query_ids`: the 128 ids are distinct.
All inputs are finite; a program needn't handle non-finite values.
Results may differ from a plain program's by a relative error of at most 0.0003.
Values may be sent and summed in bfloat16 or wider, within the bound.
No kernel may reach another device: no remote copies, remote signals or barrier semaphores. Data moves between devices by JAX's collectives and lax.ppermute only.
A program may use at most 128 MiB of HBM per device.

v0:
```python
import jax
import jax.numpy as jnp
from jax import lax
from jax.sharding import PartitionSpec as P

ITERS = 2


damping = 0.5


def broadcast(x, axis, root):
    mine = lax.axis_index(axis) == root
    return lax.psum(jnp.where(mine, x, jnp.zeros_like(x)), axis)


def symmetric(mat):
    return 0.5 * (mat + mat.T)


def solve_spd(mat, right):
    factor = jnp.linalg.cholesky(mat)
    return jax.scipy.linalg.cho_solve((factor, True), right)


def inner(left, right):
    return lax.dot_general(
        left,
        right,
        (((0,), (0,)), ((), ())),
        precision=lax.Precision.HIGHEST,
        preferred_element_type=jnp.float32,
    )


def times(left, right):
    return jnp.dot(left, right, precision=lax.Precision.HIGHEST)


def residual_sum(residual):
    return lax.psum(inner(residual, residual), "row")


def on_device(grads, seeds, bank, query_ids):
    rows = grads.shape[0]
    my_row = lax.axis_index("row")
    my_col = lax.axis_index("col")
    scale_all = jnp.exp2(seeds.astype(jnp.float32) / 4.0)
    scale_own = lax.dynamic_slice_in_dim(scale_all, my_row * rows, rows)
    bank_rows = bank.shape[0]
    local_ids = query_ids - my_row * bank_rows
    selector = (local_ids[:, None] == jnp.arange(bank_rows, dtype=jnp.int32)[None, :]).astype(
        jnp.bfloat16
    )
    picked = jnp.dot(selector, bank, preferred_element_type=jnp.float32).astype(jnp.bfloat16)
    chosen = lax.psum(picked, "row").astype(jnp.float32).astype(jnp.bfloat16)
    rhs = scale_own[:, None] * lax.dot_general(
        grads, chosen, (((1,), (1,)), ((), ())), preferred_element_type=jnp.float32
    )
    owner = my_col + 0
    panel = broadcast(grads, "row", owner)
    panel_scale = lax.dynamic_slice_in_dim(scale_all, owner * rows, rows)
    product = lax.dot_general(
        grads, panel, (((1,), (1,)), ((), ())), preferred_element_type=jnp.float32
    )
    blocks = scale_own[:, None] * product * panel_scale[None, :]
    solution = jnp.zeros_like(rhs)
    residual = rhs
    direction = rhs
    norm_now = residual_sum(residual)
    for step in range(ITERS):
        total = jnp.zeros_like(direction)
        operate_owner = my_col + 0
        other = broadcast(direction, "row", operate_owner)
        total = total + times(blocks, other)
        image = lax.psum(total, "col") + damping * direction
        curv = symmetric(lax.psum(inner(direction, image), "row"))
        alpha = solve_spd(curv, norm_now)
        solution = solution + times(direction, alpha)
        residual = residual - times(image, alpha)
        if step + 1 < ITERS:
            fresh = residual_sum(residual)
            beta = solve_spd(symmetric(norm_now), fresh)
            direction = residual + times(direction, beta)
            norm_now = fresh
    return (solution, residual)


def solution(mesh):
    placed = (P("row", None), P(), P("row", None), P())
    return jax.shard_map(
        on_device,
        mesh=mesh,
        in_specs=placed,
        out_specs=(P("row", None), P("row", None)),
        check_vma=False,
    )
```

profile of v0, /device:TPU:1, one launch (start us, length us, event | category | flops | bytes accessed | tf_op | source)
XLA Modules:
  0.0 1254.1 jit_solution(6041867342688428651)
XLA Ops:
  7.2 0.7 broadcast_subtract_fusion
  8.1 2.0 convolution_convert_fusion
  10.2 3.8 broadcast_select_fusion
  14.0 0.7 copy-done.1
  14.8 246.8 %all-reduce.25.cloned.1.call-done = (bf16[128,8192]{1,0:T(8,128)(2,1)}, bf16[512,8192]{1,0:T(8,128)(2,1)}) async-done(((bf16[128,8192]{1,0:T(8,128)(2,1)}, bf16[512,8192]{1,0:T(8,128)(2,1)}), (bf16[128,8192]{1,0:T(8,128)(2,1)}, bf16[512,8192]{1,0:T(8,128)(2,1)})) %all-reduce.25.cloned.1.call-update) | async-done | bytes 10485776 | tf_op jit(solution)/shard_map/psum | solution.py:56
  261.6 7.6 bitcast_select_fusion
  269.4 9.7 fusion
  279.1 113.6 %all-reduce.11.cloned.1.call-done = f32[512,128]{0,1:T(8,128)} async-done(((f32[512,128]{0,1:T(8,128)}), f32[512,128]{0,1:T(8,128)}) %all-reduce.11.cloned.1.call-update) | async-done | bytes 262160 | tf_op jit(solution)/shard_map/psum | solution.py:14
  392.6 2.4 fusion.37
  395.1 1.0 fusion.38
  396.1 146.8 %all-reduce.13.cloned.1.call-done = f32[512,128]{0,1:T(8,128)} async-done(((f32[512,128]{0,1:T(8,128)}), f32[512,128]{0,1:T(8,128)}) %all-reduce.13.cloned.1.call-update) | async-done | bytes 262160 | tf_op jit(solution)/shard_map/psum | solution.py:76
  542.9 2.0 fusion.3
  545.1 131.7 %all-reduce.23.cloned.1.call-done = (f32[128,128]{1,0:T(8,128)}, f32[128,128]{1,0:T(8,128)}) async-done(((f32[128,128]{1,0:T(8,128)}, f32[128,128]{1,0:T(8,128)}), (f32[128,128]{1,0:T(8,128)}, f32[128,128]{1,0:T(8,128)})) %all-reduce.23.cloned.1.call-update) | async-done | bytes 131088 | tf_op jit(solution)/shard_map/psum | solution.py:41
  676.9 0.9 copy.10
  677.8 0.9 copy.7
  678.7 0.9 fusion.24
  679.7 11.7 cholesky.59
  691.5 0.6 compare_reduce_fusion.2
  692.1 0.7 fusion.10
  692.8 9.8 custom-call.9
  702.6 1.1 fusion.27
  703.9 1.4 convolution_subtract_fusion.1
  705.3 1.0 fusion.40
  706.4 0.3 all-reduce.17.cloned.1.call-start
  706.7 11.7 cholesky.70
  718.5 0.6 compare_reduce_fusion.1
  719.1 0.7 fusion.11
  719.8 9.8 custom-call.10
  729.6 89.0 %all-reduce.15.cloned.1.call-done = f32[128,128]{1,0:T(8,128)} async-done(((f32[128,128]{1,0:T(8,128)}), f32[128,128]{1,0:T(8,128)}) %all-reduce.15.cloned.1.call-update) | async-done | bytes 65552 | tf_op jit(solution)/shard_map/psum | solution.py:41
  818.7 1.1 fusion.21
  820.0 1.1 broadcast_select_fusion.1
  821.2 123.8 %all-reduce.17.cloned.1.call-done = f32[512,128]{0,1:T(8,128)} async-done(((f32[512,128]{0,1:T(8,128)}), f32[512,128]{0,1:T(8,128)}) %all-reduce.17.cloned.1.call-update) | async-done | bytes 262160 | tf_op jit(solution)/shard_map/psum | solution.py:14
  945.0 2.4 fusion.41
  947.4 0.3 all-reduce.21.cloned.1.call-start
  947.7 147.6 %all-reduce.19.cloned.1.call-done = f32[512,128]{0,1:T(8,128)} async-done(((f32[512,128]{0,1:T(8,128)}), f32[512,128]{0,1:T(8,128)}) %all-reduce.19.cloned.1.call-update) | async-done | bytes 262160 | tf_op jit(solution)/shard_map/psum | solution.py:76
  1095.2 2.0 fusion.5
  1097.2 0.6 fusion.39
  1097.8 119.8 %all-reduce.21.cloned.1.call-done = f32[128,128]{1,0:T(8,128)} async-done(((f32[128,128]{1,0:T(8,128)}), f32[128,128]{1,0:T(8,128)}) %all-reduce.21.cloned.1.call-update) | async-done | bytes 65552 | tf_op jit(solution)/shard_map/psum | solution.py:77
  1217.7 0.9 copy.14
  1218.6 0.9 fusion.18
  1219.6 11.7 cholesky.81
  1231.3 0.6 compare_reduce_fusion
  1232.0 0.7 fusion.12
  1232.6 9.8 custom-call.11
  1242.4 1.1 fusion.15
  1243.8 1.3 convolution_add_fusion
  1245.1 1.4 convolution_subtract_fusion
  1246.4 0.8 copy.17
  (31 shorter events, 1.9 us)
Async XLA Ops:
  7.2 1.0 copy-start
  7.2 254.5 %all-reduce.25.cloned.1.call-start = ((), (), s32[]{:S(2)}) async-start(), calls=%async_computation.7 | async-start | bytes 20971520 | tf_op jit(solution)/shard_map/psum | solution.py:56
  13.9 0.8 copy-start.1
  13.9 378.7 %all-reduce.11.cloned.1.call-start = ((), (), s32[]{:S(2)}) async-start(), calls=%async_computation | async-start | bytes 524288 | tf_op jit(solution)/shard_map/psum | solution.py:14
  269.3 273.6 %all-reduce.13.cloned.1.call-start = ((), (), s32[]{:S(2)}) async-start(), calls=%async_computation.1 | async-start | bytes 524288 | tf_op jit(solution)/shard_map/psum | solution.py:76
  395.0 281.8 %all-reduce.23.cloned.1.call-start = ((), (), s32[]{:S(2)}) async-start(), calls=%async_computation.6 | async-start | bytes 262144 | tf_op jit(solution)/shard_map/psum | solution.py:41
  544.9 273.7 %all-reduce.15.cloned.1.call-start = ((), (), s32[]{:S(2)}) async-start(), calls=%async_computation.2 | async-start | bytes 131072 | tf_op jit(solution)/shard_map/psum | solution.py:41
  706.4 238.6 %all-reduce.17.cloned.1.call-start = ((), (), s32[]{:S(2)}) async-start(), calls=%async_computation.3 | async-start | bytes 524288 | tf_op jit(solution)/shard_map/psum | solution.py:14
  821.1 274.1 %all-reduce.19.cloned.1.call-start = ((), (), s32[]{:S(2)}) async-start(), calls=%async_computation.4 | async-start | bytes 524288 | tf_op jit(solution)/shard_map/psum | solution.py:76
  947.4 270.3 %all-reduce.21.cloned.1.call-start = ((), (), s32[]{:S(2)}) async-start(), calls=%async_computation.5 | async-start | bytes 131072 | tf_op jit(solution)/shard_map/psum | solution.py:77
Sparse Core Ops, SparseCore 0:
  14.1 247.5 all-reduce.24
  269.4 123.1 all-reduce.10
  395.8 147.0 all-reduce.12
  546.0 130.8 all-reduce.22
  706.5 112.1 all-reduce.14
  821.7 123.2 all-reduce.16
  948.1 147.0 all-reduce.18
  1098.4 119.1 all-reduce.20
where the time goes:
time: 1260 us; the launch traced here: 1250 us
  waiting for transfers between devices  1120 us (89%)
  other arithmetic  74.8 us (6%)
  matrix products  39.8 us (3%)
  between operations  14.4 us (1%)
    psum x2, waiting for transfers between devices, on_device(): image = lax.psum(total, 'col') + damping * direction  294 us
    psum x1, waiting for transfers between devices, on_device(): chosen = lax.psum(picked, 'row').astype(jnp.float32).astype(jnp.bfloat16)  247 us
    psum x2, waiting for transfers between devices, broadcast(): return lax.psum(jnp.where(mine, x, jnp.zeros_like(x)), axis)  237 us
    psum x2, waiting for transfers between devices, residual_sum(): return lax.psum(inner(residual, residual), 'row')  221 us
    psum x1, waiting for transfers between devices, on_device(): curv = symmetric(lax.psum(inner(direction, image), 'row'))  120 us
    another operation x9, other arithmetic, solve_spd(): factor = jnp.linalg.cholesky(mat)  37.2 us
    another operation x6, other arithmetic, solve_spd(): return jax.scipy.linalg.cho_solve((factor, True), right)  31.4 us
  transfers between devices with their start and end apart: 8, of which 8 were waited for; matrix products, arithmetic and copies ran while one was open for 3% of the time, Pallas kernels for 0%

commit v1 on v0

v1 whole, which is shorter than its diff:
```python
import jax
import jax.numpy as jnp
from jax import lax
from jax.sharding import PartitionSpec as P

damping = 0.5


def symmetric(mat):
    return 0.5 * (mat + mat.T)


def solve_spd(mat, right):
    factor = jnp.linalg.cholesky(mat)
    return jax.scipy.linalg.cho_solve((factor, True), right)


def full(left, right, dims=((1,), (0,))):
    return lax.dot_general(
        left,
        right,
        (dims, ((), ())),
        precision=lax.Precision.HIGHEST,
        preferred_element_type=jnp.float32,
    )


def two_terms(value):
    high = lax.reduce_precision(value, 8, 7)
    return jnp.concatenate([high, value - high]).astype(jnp.bfloat16)


def swap(pieces, axis):
    return lax.all_to_all(pieces, axis, 0, 0, tiled=True)


def spread(piece, axis, size):
    return swap(jnp.broadcast_to(piece[None], (size,) + piece.shape), axis)


def split_last(value, parts):
    lead, last = value.shape
    return value.reshape(lead, parts, last // parts).transpose(1, 0, 2)


def join_last(pieces):
    parts, lead, last = pieces.shape
    return pieces.transpose(1, 0, 2).reshape(lead, parts * last)


def on_device(rows_n, cols_n, grads, seeds, bank, query_ids):
    rows, depth = grads.shape
    queries = query_ids.shape[0]
    mine = queries // cols_n
    my_row = lax.axis_index("row")
    my_col = lax.axis_index("col")
    own_seeds = lax.dynamic_slice_in_dim(seeds, my_row * rows, rows)
    scale = jnp.exp2(own_seeds.astype(jnp.float32) / 4.0)[None, :]

    def project(value):
        both = lax.dot_general(
            two_terms(value), grads, (((1,), (1,)), ((), ())), preferred_element_type=jnp.float32
        )
        return scale * (both[:mine] + both[mine:])

    def gather_back(value):
        both = lax.dot_general(
            two_terms(scale * value), grads, (((1,), (0,)), ((), ())), preferred_element_type=jnp.float32
        )
        part = both[:mine] + both[mine:]
        piece = jnp.sum(swap(split_last(part, rows_n), "row"), axis=0)
        return join_last(spread(piece, "row", rows_n))

    bank_rows = bank.shape[0]
    ids = lax.dynamic_slice_in_dim(query_ids, my_col * mine, mine) - my_row * bank_rows
    selector = (ids[:, None] == jnp.arange(bank_rows, dtype=jnp.int32)[None, :]).astype(jnp.bfloat16)
    picked = jnp.dot(selector, bank, preferred_element_type=jnp.float32).astype(jnp.bfloat16)
    arrived = swap(split_last(picked, rows_n), "row").astype(jnp.float32)
    piece = jnp.sum(arrived, axis=0).astype(jnp.bfloat16)
    chosen = join_last(spread(piece, "row", rows_n))

    base = scale * lax.dot_general(
        chosen, grads, (((1,), (1,)), ((), ())), preferred_element_type=jnp.float32
    )
    back = gather_back(base)
    wide = chosen.astype(jnp.float32)
    square = jnp.sum(wide * back, axis=1, keepdims=True)
    curve = jnp.sum(back * back, axis=1, keepdims=True) + damping * square
    step = square / curve
    other = base - step * (project(back) + damping * base)
    other_image = project(gather_back(other)) + damping * other

    lanes = 128
    message = jnp.concatenate(
        [base, other, other_image, jnp.broadcast_to(step, (mine, lanes))], axis=1
    )
    held = spread(message, "col", cols_n).reshape(queries, 3 * rows + lanes)
    base, other, other_image = held[:, :rows], held[:, rows : 2 * rows], held[:, 2 * rows : 3 * rows]
    step = held[:, 3 * rows]

    last = ((1,), (1,))
    moments = jnp.concatenate(
        [
            full(base, base, last),
            full(base, other, last),
            full(other, other, last),
            full(other, other_image, last),
        ]
    )
    piece = jnp.sum(swap(moments.reshape(rows_n, -1, queries), "row"), axis=0)
    moments = spread(piece, "row", rows_n).reshape(4, queries, queries)
    bb, bt, tt, tat = moments[0], moments[1], moments[2], symmetric(moments[3])

    bab = symmetric((bb - bt) / step[None, :])
    tab = (bt.T - tt) / step[None, :]
    alpha = solve_spd(bab, bb)
    second = alpha / step[:, None]
    first = jnp.eye(queries, dtype=jnp.float32) - second

    def quad(left, a, b, c, right):
        cross = full(left.T, full(b, right))
        return full(left.T, full(a, left)) + cross + cross.T + full(right.T, full(c, right))

    fresh = quad(first, bb, bt, tt, second)
    beta = solve_spd(symmetric(bb), fresh)
    mixed = first + beta
    curv = symmetric(quad(mixed, bab, tab.T, tat, second))
    alpha_next = solve_spd(curv, fresh)
    gain = full(mixed, alpha_next)
    gain_other = full(second, alpha_next)
    shift = gain / step[:, None]
    lead = ((0,), (0,))
    solution = full(base, alpha + gain, lead) + full(other, gain_other, lead)
    residual = (
        full(base, first - shift, lead)
        + full(other, second + shift, lead)
        - full(other_image, gain_other, lead)
    )
    return (solution, residual)


def solution(mesh):
    placed = (P("row", None), P(), P("row", None), P())

    def body(*args):
        return on_device(mesh.shape["row"], mesh.shape["col"], *args)

    return jax.shard_map(
        body,
        mesh=mesh,
        in_specs=placed,
        out_specs=(P("row", None), P("row", None)),
        check_vma=False,
    )
```

time: 1260 us -> 244 us (0.19)
  waiting for transfers between devices: 1120 us -> 12.3 us
  blocking collectives: 0 us -> 100 us
  between operations: 14.4 us -> 1.36 us
    psum x8 -> x0, waiting for transfers between devices: 1120 us -> none  [the longest x2 294 us: on_device(): image = lax.psum(total, 'col') + damping * direction]
    all_to_all x0 -> x7, blocking collectives: none -> 100 us  [swap(): return lax.all_to_all(pieces, axis, 0, 0, tiled=True)]
    dot_general x13 -> x28, matrix products: 33.8 us -> 33 us  [the longest x2 11.3 us: project(): lax.dot_general(two_terms(value), grads, (((1,), (1,)), ((), ())), prefer...]
  transfers between devices with their start and end apart: 8 -> 2, of which waited for: 8 -> 2; matrix products, arithmetic and copies ran while one was open for 3% -> 0% of each run, Pallas kernels for 0% -> 0%
where the time goes in v1:
time: 244 us; the launch traced here: 240 us
  blocking collectives  100 us (41%)
  other arithmetic  79.9 us (33%)
  matrix products  34.6 us (14%)
  waiting for transfers between devices  12.3 us (5%)
  starting transfers between devices  8.46 us (3%)
  local copies, waits for them, and re-layouts  2.95 us (1%)
    all_to_all x7, blocking collectives, swap(): return lax.all_to_all(pieces, axis, 0, 0, tiled=True)  100 us
    another operation x6, other arithmetic, solve_spd(): return jax.scipy.linalg.cho_solve((factor, True), right)  40.5 us
    another operation x9, other arithmetic, solve_spd(): factor = jnp.linalg.cholesky(mat)  37.2 us
    all_to_all x2, waiting for transfers between devices, swap(): return lax.all_to_all(pieces, axis, 0, 0, tiled=True)  12.3 us
    dot_general x2, matrix products, project(): lax.dot_general(two_terms(value), grads, (((1,), (1,)), ((), ())), prefer...  11.3 us
    dot_general x23, matrix products, full(): lax.dot_general(left, right, (dims, ((), ())), precision=lax.Precision.HI...  10.1 us
    all_to_all x2, starting transfers between devices, swap(): return lax.all_to_all(pieces, axis, 0, 0, tiled=True)  8.46 us
    dot_general x1, matrix products, on_device(): lax.dot_general(chosen, grads, (((1,), (1,)), ((), ())), preferred_elemen...  5.79 us
  transfers between devices with their start and end apart: 2, of which 2 were waited for; matrix products, arithmetic and copies ran while one was open for 0% of the time, Pallas kernels for 0%

profile of v1, /device:TPU:1, one launch (start us, length us, event | category | flops | bytes accessed | tf_op | source)
XLA Modules:
  0.0 239.7 jit_solution(6893200565599975200)
XLA Ops:
  0.7 0.8 dynamic-slice_subtract_fusion
  1.8 12.8 %all_to_all.45 = bf16[16,8,512]{2,1,0:T(8,128)(2,1)S(1)} all-to-all(bf16[16,8,512]{2,1,0:T(8,128)(2,1)S(1)} %bitcast.160), channel_id=1, replica_groups=mesh['row'=16,'col'=16] {'row'}, dimensions={0} | all-to-all | bytes 262144 | tf_op jit(solution)/shard_map/all_to_all | solution.py:34
  14.7 0.7 broadcast_in_dim.12
  15.3 4.0 %all-to-all-start.1 = ((bf16[16,8,512]{2,1,0:T(8,128)(2,1)}), bf16[16,8,512]{2,1,0:T(8,128)(2,1)S(1)}, u32[]{:S(2)}, u32[]{:S(2)}) async-start(bf16[16,8,512]{2,1,0:T(8,128)(2,1)} %broadcast_in_dim.12), calls=%async_computation.1 | async-start | bytes 262144 | tf_op jit(solution)/shard_map/all_to_all | solution.py:34
  19.3 0.8 multiply_exponential_fusion
  20.1 5.4 %all-to-all-done.1 = bf16[16,8,512]{2,1,0:T(8,128)(2,1)S(1)} async-done(((bf16[16,8,512]{2,1,0:T(8,128)(2,1)}), bf16[16,8,512]{2,1,0:T(8,128)(2,1)S(1)}, u32[]{:S(2)}, u32[]{:S(2)}) %all-to-all-start.1) | async-done | bytes 131104 | tf_op jit(solution)/shard_map/all_to_all | solution.py:34
  25.5 5.8 %reduce-precision_convert_fusion.3 = (bf16[8,512]{1,0:T(8,128)(2,1)S(1)}, bf16[8,512]{1,0:T(8,128)(2,1)S(1)}, f32[8,512]{1,0:T(8,128)S(1)}) fusion(f32[512]{0:T(512)S(1)} %multiply_exponential_fusion, bf16[8,8192]{1,0:T(8,128)(2,1)S(1)} %bitcast.152, bf16[512,8192]{1,0:T(8,128)(2,1)} %param.7), kind=kOutput, calls=%fused_computation.107 | convolution fusion | flops 67133440 | bytes 8554496 | tf_op jit(solution)/shard_map/dot_general | solution.py:82
  31.3 1.2 fusion.77
  32.6 10.4 %all_to_all.46 = f32[16,8,512]{2,1,0:T(8,128)S(1)} all-to-all(f32[16,8,512]{2,1,0:T(8,128)S(1)} %bitcast.153), channel_id=1, replica_groups=mesh['row'=16,'col'=16] {'row'}, dimensions={0} | all-to-all | bytes 524288 | tf_op jit(solution)/shard_map/all_to_all | solution.py:34
  43.0 10.6 %all_to_all.47 = f32[16,8,512]{2,1,0:T(8,128)S(1)} all-to-all(f32[16,8,512]{2,1,0:T(8,128)S(1)} %broadcast_in_dim.13), channel_id=1, replica_groups=mesh['row'=16,'col'=16] {'row'}, dimensions={0} | all-to-all | bytes 524288 | tf_op jit(solution)/shard_map/all_to_all | solution.py:34
  53.8 5.7 %fusion.3 = f32[16,512]{1,0:T(8,128)S(1)} fusion(bf16[512,8192]{1,0:T(8,128)(2,1)} %param.7, bf16[8,8192]{1,0:T(8,128)(2,1)S(1)} %get-tuple-element.15, bf16[8,8192]{1,0:T(8,128)(2,1)S(1)} %get-tuple-element.14), kind=kOutput, calls=%fused_computation.17 | convolution fusion | flops 134742016 | bytes 8683520 | tf_op jit(solution)/shard_map/dot_general | solution.py:61
  59.6 4.6 %fusion.81 = f32[16,8192]{1,0:T(8,128)S(1)} fusion(bf16[512,8192]{1,0:T(8,128)(2,1)} %param.7, bf16[8,512]{1,0:T(8,128)(2,1)S(1)} %fusion.70, bf16[8,512]{1,0:T(8,128)(2,1)S(1)} %get-tuple-element.6), kind=kOutput, calls=%fused_computation.122 | convolution fusion | flops 134250496 | bytes 8929280 | tf_op jit(solution)/shard_map/dot_general | solution.py:67
  64.2 10.6 %all_to_all.48 = f32[16,8,512]{2,1,0:T(8,128)S(1)} all-to-all(f32[16,8,512]{2,1,0:T(8,128)S(1)} %bitcast.154), channel_id=1, replica_groups=mesh['row'=16,'col'=16] {'row'}, dimensions={0} | all-to-all | bytes 524288 | tf_op jit(solution)/shard_map/all_to_all | solution.py:34
  74.9 10.6 %all_to_all.49 = f32[16,8,512]{2,1,0:T(8,128)S(1)} all-to-all(f32[16,8,512]{2,1,0:T(8,128)S(1)} %broadcast_in_dim.14), channel_id=1, replica_groups=mesh['row'=16,'col'=16] {'row'}, dimensions={0} | all-to-all | bytes 524288 | tf_op jit(solution)/shard_map/all_to_all | solution.py:34
  85.6 5.6 %fusion.7 = f32[16,512]{1,0:T(8,128)S(1)} fusion(bf16[512,8192]{1,0:T(8,128)(2,1)} %param.7, bf16[8,8192]{1,0:T(8,128)(2,1)S(1)} %get-tuple-element.13, bf16[8,8192]{1,0:T(8,128)(2,1)S(1)} %get-tuple-element.12), kind=kOutput, calls=%fused_computation.21 | convolution fusion | flops 134742016 | bytes 8683520 | tf_op jit(solution)/shard_map/dot_general | solution.py:61
  91.4 32.4 %all_to_all.50 = f32[16,8,1664]{2,1,0:T(8,128)S(1)} all-to-all(f32[16,8,1664]{2,1,0:T(8,128)S(1)} %broadcast_in_dim.16), channel_id=1, replica_groups=mesh['row'=16,'col'=16] {'col'}, dimensions={0} | all-to-all | bytes 1703936 | tf_op jit(solution)/shard_map/all_to_all | solution.py:34
  123.8 0.4 fusion.20
  124.2 0.4 fusion.14
  124.6 0.4 fusion.27
  124.9 0.4 fusion.22
  125.3 12.6 %all_to_all.51 = f32[16,32,128]{2,1,0:T(8,128)S(1)} all-to-all(f32[16,32,128]{2,1,0:T(8,128)S(1)} %bitcast.155), channel_id=1, replica_groups=mesh['row'=16,'col'=16] {'row'}, dimensions={0} | all-to-all | bytes 524288 | tf_op jit(solution)/shard_map/all_to_all | solution.py:34
  137.9 0.7 broadcast_in_dim.17
  138.7 4.5 %all-to-all-start.8 = ((f32[16,32,128]{2,1,0:T(8,128)}), f32[16,32,128]{2,1,0:T(8,128)S(1)}, u32[]{:S(2)}, u32[]{:S(2)}) async-start(f32[16,32,128]{2,1,0:T(8,128)} %broadcast_in_dim.17), calls=%async_computation.8 | async-start | bytes 524288 | tf_op jit(solution)/shard_map/all_to_all | solution.py:34
  143.3 6.9 %all-to-all-done.8 = f32[16,32,128]{2,1,0:T(8,128)S(1)} async-done(((f32[16,32,128]{2,1,0:T(8,128)}), f32[16,32,128]{2,1,0:T(8,128)S(1)}, u32[]{:S(2)}, u32[]{:S(2)}) %all-to-all-start.8) | async-done | bytes 262176 | tf_op jit(solution)/shard_map/all_to_all | solution.py:34
  150.6 11.7 %cholesky.59 = f32[128,128]{1,0:T(8,128)S(1)} custom-call(f32[128,128]{1,0:T(8,128)S(1)} %copy.53), custom_call_target="Cholesky" | custom-call | tf_op jit(solution)/shard_map/jit(cholesky)/cholesky | solution.py:14
  162.3 0.6 compare_reduce_fusion.2
  163.0 0.7 fusion.30
  163.6 9.8 %custom-call.9 = f32[1,128,128]{1,2,0:T(8,128)S(1)} custom-call(f32[1,128,128]{2,1,0:T(8,128)S(1)} %fusion.30), custom_call_target="InvertDiagBlocksLowerTriangular" | custom-call | tf_op jit(solution)/shard_map/jit(_cho_solve)/triangular_solve | solution.py:15
  173.4 0.3 fusion.53
  174.7 0.4 fusion.63
  175.4 0.3 fusion.45
  175.9 0.3 fusion.92
  176.3 0.4 fusion.91
  176.8 11.7 %cholesky.70 = f32[128,128]{1,0:T(8,128)S(1)} custom-call(f32[128,128]{1,0:T(8,128)S(1)} %fusion.50), custom_call_target="Cholesky" | custom-call | tf_op jit(solution)/shard_map/jit(cholesky)/cholesky | solution.py:14
  188.6 0.6 compare_reduce_fusion.1
  189.2 0.7 fusion.31
  189.9 18.9 %custom-call.10 = f32[1,128,128]{1,2,0:T(8,128)S(1)} custom-call(f32[1,128,128]{2,1,0:T(8,128)S(1)} %fusion.31), custom_call_target="InvertDiagBlocksLowerTriangular" | custom-call | tf_op jit(solution)/shard_map/jit(_cho_solve)/triangular_solve | solution.py:15
  208.8 0.4 fusion
  209.2 0.4 convolution_add_fusion.3
  211.2 11.7 %cholesky.81 = f32[128,128]{1,0:T(8,128)S(1)} custom-call(f32[128,128]{1,0:T(8,128)S(1)} %fusion.39), custom_call_target="Cholesky" | custom-call | tf_op jit(solution)/shard_map/jit(cholesky)/cholesky | solution.py:14
  222.9 0.6 compare_reduce_fusion
  223.6 0.7 fusion.32
  224.3 9.8 %custom-call.11 = f32[1,128,128]{1,2,0:T(8,128)S(1)} custom-call(f32[1,128,128]{2,1,0:T(8,128)S(1)} %fusion.32), custom_call_target="InvertDiagBlocksLowerTriangular" | custom-call | tf_op jit(solution)/shard_map/jit(_cho_solve)/triangular_solve | solution.py:15
  235.1 0.6 fusion.16
  235.7 0.6 fusion.18
  236.3 0.6 convolution_add_fusion
  236.9 1.3 convolution_subtract_fusion
  238.2 1.3 convolution_add_fusion.1
  (61 shorter events, 5.8 us)
Async XLA Ops:
  0.6 1.0 copy-start
  15.3 10.2 %all-to-all-start.1 = ((bf16[16,8,512]{2,1,0:T(8,128)(2,1)}), bf16[16,8,512]{2,1,0:T(8,128)(2,1)S(1)}, u32[]{:S(2)}, u32[]{:S(2)}) async-start(bf16[16,8,512]{2,1,0:T(8,128)(2,1)} %broadcast_in_dim.12), calls=%async_computation.1 | async-start | bytes 262144 | tf_op jit(solution)/shard_map/all_to_all | solution.py:34
  25.5 5.8 %copy-start.1 = (bf16[512,8192]{1,0:T(8,128)(2,1)S(1)}, bf16[512,8192]{1,0:T(8,128)(2,1)}, u32[]{:S(2)}) copy-start(bf16[512,8192]{1,0:T(8,128)(2,1)} %param.7) | copy-start | bytes 25165828
  138.7 11.5 %all-to-all-start.8 = ((f32[16,32,128]{2,1,0:T(8,128)}), f32[16,32,128]{2,1,0:T(8,128)S(1)}, u32[]{:S(2)}, u32[]{:S(2)}) async-start(f32[16,32,128]{2,1,0:T(8,128)} %broadcast_in_dim.17), calls=%async_computation.8 | async-start | bytes 524288 | tf_op jit(solution)/shard_map/all_to_all | solution.py:34

commit v2 on v1

--- a/solution.py
+++ b/solution.py
@@ -1,18 +1,13 @@
+import functools
+
 import jax
 import jax.numpy as jnp
 from jax import lax
+from jax.experimental import pallas as pl
+from jax.experimental.pallas import tpu as pltpu
 from jax.sharding import PartitionSpec as P
 
 damping = 0.5
-
-
-def symmetric(mat):
-    return 0.5 * (mat + mat.T)
-
-
-def solve_spd(mat, right):
-    factor = jnp.linalg.cholesky(mat)
-    return jax.scipy.linalg.cho_solve((factor, True), right)
 
 
 def full(left, right, dims=((1,), (0,))):
@@ -46,6 +41,115 @@
 def join_last(pieces):
     parts, lead, last = pieces.shape
     return pieces.transpose(1, 0, 2).reshape(lead, parts * last)
+
+
+def moments_kernel(rows, held_ref, out_ref):
+    base = held_ref[:, :rows]
+    other = held_ref[:, rows : 2 * rows]
+    image = held_ref[:, 2 * rows : 3 * rows]
+    queries = base.shape[0]
+    last = ((1,), (1,))
+    out_ref[:queries] = full(base, base, last)
+    out_ref[queries : 2 * queries] = full(other, base, last)
+    out_ref[2 * queries : 3 * queries] = full(other, other, last)
+    out_ref[3 * queries :] = full(other, image, last)
+
+
+def moments_of(held, rows):
+    queries = held.shape[0]
+    return pl.pallas_call(
+        functools.partial(moments_kernel, rows),
+        out_shape=jax.ShapeDtypeStruct((4 * queries, queries), jnp.float32),
+    )(held)
+
+
+def reduce_moments(moments, rows_n):
+    queries = moments.shape[1]
+    piece = jnp.sum(swap(moments.reshape(rows_n, -1, queries), "row"), axis=0)
+    return spread(piece, "row", rows_n).reshape(4 * queries, queries)
+
+
+def inverse_spd(mat, eye, inv_ref, left_ref):
+    on_diag = mat * eye
+    across = lax.rsqrt(jnp.sum(on_diag, axis=0, keepdims=True))
+    down = lax.rsqrt(jnp.sum(on_diag, axis=1, keepdims=True))
+    unit = mat * across * down
+    reach = jnp.sum(jnp.abs(unit), axis=1, keepdims=True)
+    share = 1.0 / jnp.max(reach, axis=0, keepdims=True)
+    left = eye - share * unit
+    inv = share * (eye + left)
+    left = full(left, left)
+    for _ in range(4):
+        inv, left = inv + full(inv, left), full(left, left)
+    inv_ref[...] = inv
+    left_ref[...] = left
+
+    def open_still(state):
+        count, size = state
+        return jnp.logical_and(count < 40, size > 1e-5)
+
+    def again(state):
+        inv, left = inv_ref[...], left_ref[...]
+        inv_ref[...] = inv + full(inv, left)
+        left = full(left, left)
+        left_ref[...] = left
+        return state[0] + 1, jnp.sum(left * left)
+
+    lax.while_loop(open_still, again, (0, jnp.sum(left * left)))
+    inv = inv_ref[...]
+    inv = inv + full(inv, left_ref[...])
+    return inv * across * down
+
+
+def solve_with(mat, inv, right):
+    first = full(inv, right)
+    return first + full(inv, right - full(mat, first))
+
+
+def finish_kernel(rows, held_ref, moments_ref, solution_ref, residual_ref, inv_ref, left_ref):
+    queries = held_ref.shape[0]
+    bb = moments_ref[:queries]
+    tb = moments_ref[queries : 2 * queries]
+    tt = moments_ref[2 * queries : 3 * queries]
+    tat = moments_ref[3 * queries :]
+    per_step = 1.0 / held_ref[:, 3 * rows :]
+    shape = (queries, queries)
+    row_id = lax.broadcasted_iota(jnp.int32, shape, 0)
+    eye = jnp.where(row_id == lax.broadcasted_iota(jnp.int32, shape, 1), 1.0, 0.0)
+
+    bab = per_step * (bb - tb)
+    bat = per_step * (tb.T - tt)
+    tab = bat.T
+    inv = inverse_spd(bab, eye, inv_ref, left_ref)
+    alpha = solve_with(bab, inv, bb)
+    second = per_step * alpha
+    second_t = second.T
+    first = eye - second
+    fresh = full(second_t, tb - full(tab, alpha))
+    mixed = -solve_with(bab, inv, full(bat, second))
+    curv = full(second_t, full(tab, mixed) + full(tat, second))
+    curv = 0.5 * (curv + curv.T)
+    inv = inverse_spd(curv, eye, inv_ref, left_ref)
+    alpha_next = solve_with(curv, inv, fresh)
+    gain = full(mixed, alpha_next)
+    gain_other = full(second, alpha_next)
+    shift = per_step * gain
+
+    base = held_ref[:, :rows].T
+    other = held_ref[:, rows : 2 * rows].T
+    image = held_ref[:, 2 * rows : 3 * rows].T
+    solution_ref[...] = full(base, alpha + gain) + full(other, gain_other)
+    residual_ref[...] = full(base, first - shift) + full(other, second + shift) - full(image, gain_other)
+
+
+def finish(held, moments, rows):
+    queries = held.shape[0]
+    shape = jax.ShapeDtypeStruct((rows, queries), jnp.float32)
+    return pl.pallas_call(
+        functools.partial(finish_kernel, rows),
+        out_shape=(shape, shape),
+        scratch_shapes=[pltpu.VMEM((queries, queries), jnp.float32)] * 2,
+    )(held, moments)
 
 
 def on_device(rows_n, cols_n, grads, seeds, bank, query_ids):
@@ -95,48 +199,7 @@
         [base, other, other_image, jnp.broadcast_to(step, (mine, lanes))], axis=1
     )
     held = spread(message, "col", cols_n).reshape(queries, 3 * rows + lanes)
-    base, other, other_image = held[:, :rows], held[:, rows : 2 * rows], held[:, 2 * rows : 3 * rows]
-    step = held[:, 3 * rows]
-
-    last = ((1,), (1,))
-    moments = jnp.concatenate(
-        [
-            full(base, base, last),
-            full(base, other, last),
-            full(other, other, last),
-            full(other, other_image, last),
-        ]
-    )
-    piece = jnp.sum(swap(moments.reshape(rows_n, -1, queries), "row"), axis=0)
-    moments = spread(piece, "row", rows_n).reshape(4, queries, queries)
-    bb, bt, tt, tat = moments[0], moments[1], moments[2], symmetric(moments[3])
-
-    bab = symmetric((bb - bt) / step[None, :])
-    tab = (bt.T - tt) / step[None, :]
-    alpha = solve_spd(bab, bb)
-    second = alpha / step[:, None]
-    first = jnp.eye(queries, dtype=jnp.float32) - second
-
-    def quad(left, a, b, c, right):
-        cross = full(left.T, full(b, right))
-        return full(left.T, full(a, left)) + cross + cross.T + full(right.T, full(c, right))
-
-    fresh = quad(first, bb, bt, tt, second)
-    beta = solve_spd(symmetric(bb), fresh)
-    mixed = first + beta
-    curv = symmetric(quad(mixed, bab, tab.T, tat, second))
-    alpha_next = solve_spd(curv, fresh)
-    gain = full(mixed, alpha_next)
-    gain_other = full(second, alpha_next)
-    shift = gain / step[:, None]
-    lead = ((0,), (0,))
-    solution = full(base, alpha + gain, lead) + full(other, gain_other, lead)
-    residual = (
-        full(base, first - shift, lead)
-        + full(other, second + shift, lead)
-        - full(other_image, gain_other, lead)
-    )
-    return (solution, residual)
+    return finish(held, reduce_moments(moments_of(held, rows), rows_n), rows)
 
 
 def solution(mesh):

time: 244 us -> 165 us (0.68); the launches traced: 240 us -> 164 us
  other arithmetic: 79.9 us -> 2.1 us
  Pallas kernels: 0 us -> 15.5 us
  blocking collectives: 100 us -> 112 us
  matrix products: 34.6 us -> 23.1 us
  waiting for transfers between devices: 12.3 us -> 5.44 us
  starting transfers between devices: 8.46 us -> 3.96 us
    another operation x19 -> x4, other arithmetic: 77.8 us -> 0.16 us  [the longest x6 40.5 us: solve_spd(): return jax.scipy.linalg.cho_solve((factor, True), right)]
    pallas_call x0 -> x2, Pallas kernels: none -> 15.5 us  [the longest x1 12.7 us: finish(): pl.pallas_call(functools.partial(finish_kernel, rows), out_shape=(shape,...]
    all_to_all x7 -> x8, blocking collectives: 100 us -> 112 us  [swap(): return lax.all_to_all(pieces, axis, 0, 0, tiled=True)]
    dot_general x23 -> x0, matrix products: 10.1 us -> none  [full(): lax.dot_general(left, right, (dims, ((), ())), precision=lax.Precision.HI...]
    all_to_all x2 -> x1, waiting for transfers between devices: 12.3 us -> 5.44 us  [swap(): return lax.all_to_all(pieces, axis, 0, 0, tiled=True)]
    all_to_all x2 -> x1, starting transfers between devices: 8.46 us -> 3.96 us  [swap(): return lax.all_to_all(pieces, axis, 0, 0, tiled=True)]
  transfers between devices with their start and end apart: 2 -> 1, of which waited for: 2 -> 1; matrix products, arithmetic and copies ran while one was open for 0% -> 0% of each run, Pallas kernels for 0% -> 0%
where the time goes in v2:
time: 165 us; the launch traced here: 164 us
  blocking collectives  112 us (68%)
  matrix products  23.1 us (14%)
  Pallas kernels  15.5 us (9%)
  waiting for transfers between devices  5.44 us (3%)
  starting transfers between devices  3.96 us (2%)
  other arithmetic  2.1 us (1%)
    all_to_all x8, blocking collectives, swap(): return lax.all_to_all(pieces, axis, 0, 0, tiled=True)  112 us
    pallas_call x1, Pallas kernels, finish(): pl.pallas_call(functools.partial(finish_kernel, rows), out_shape=(shape,...  12.7 us
    dot_general x2, matrix products, project(): lax.dot_general(two_terms(value), grads, (((1,), (1,)), ((), ())), prefer...  11.3 us
    dot_general x1, matrix products, on_device(): lax.dot_general(chosen, grads, (((1,), (1,)), ((), ())), preferred_elemen...  5.79 us
    dot_general x2, matrix products, gather_back(): lax.dot_general(two_terms(scale * value), grads, (((1,), (0,)), ((), ()))...  5.79 us
    all_to_all x1, waiting for transfers between devices, swap(): return lax.all_to_all(pieces, axis, 0, 0, tiled=True)  5.44 us
    all_to_all x1, starting transfers between devices, swap(): return lax.all_to_all(pieces, axis, 0, 0, tiled=True)  3.96 us
  transfers between devices with their start and end apart: 1, of which 1 were waited for; matrix products, arithmetic and copies ran while one was open for 0% of the time, Pallas kernels for 0%

profile of v2, /device:TPU:1, one launch (start us, length us, event | category | flops | bytes accessed | tf_op | source)
XLA Modules:
  0.0 164.2 jit_solution(14496051103367453547)
XLA Ops:
  0.6 0.0 copy-start
  0.7 0.8 dynamic-slice_subtract_fusion
  1.4 0.2 copy-done
  1.6 0.2 convolution_convert_fusion
  1.8 12.8 %all_to_all.45 = bf16[16,8,512]{2,1,0:T(8,128)(2,1)S(1)} all-to-all(bf16[16,8,512]{2,1,0:T(8,128)(2,1)S(1)} %bitcast.44), channel_id=1, replica_groups=mesh['row'=16,'col'=16] {'row'}, dimensions={0} | all-to-all | bytes 262144 | tf_op jit(solution)/shard_map/all_to_all | solution.py:29
  14.7 0.7 broadcast_in_dim.12
  15.3 4.0 %all-to-all-start.1 = ((bf16[16,8,512]{2,1,0:T(8,128)(2,1)}), bf16[16,8,512]{2,1,0:T(8,128)(2,1)S(1)}, u32[]{:S(2)}, u32[]{:S(2)}) async-start(bf16[16,8,512]{2,1,0:T(8,128)(2,1)} %broadcast_in_dim.12), calls=%async_computation.1 | async-start | bytes 262144 | tf_op jit(solution)/shard_map/all_to_all | solution.py:29
  19.3 0.8 multiply_exponential_fusion
  20.1 5.4 %all-to-all-done.1 = bf16[16,8,512]{2,1,0:T(8,128)(2,1)S(1)} async-done(((bf16[16,8,512]{2,1,0:T(8,128)(2,1)}), bf16[16,8,512]{2,1,0:T(8,128)(2,1)S(1)}, u32[]{:S(2)}, u32[]{:S(2)}) %all-to-all-start.1) | async-done | bytes 131104 | tf_op jit(solution)/shard_map/all_to_all | solution.py:29
  25.5 0.0 copy-start.1
  25.5 5.8 %reduce-precision_convert_fusion.3 = (bf16[8,512]{1,0:T(8,128)(2,1)S(1)}, bf16[8,512]{1,0:T(8,128)(2,1)S(1)}, f32[8,512]{1,0:T(8,128)S(1)}) fusion(f32[512]{0:T(512)S(1)} %multiply_exponential_fusion, bf16[8,8192]{1,0:T(8,128)(2,1)S(1)} %bitcast.38, bf16[512,8192]{1,0:T(8,128)(2,1)} %param.4), kind=kOutput, calls=%fused_computation.26 | convolution fusion | flops 67133440 | bytes 8554496 | tf_op jit(solution)/shard_map/dot_general | solution.py:186
  31.3 0.0 copy-done.1
  31.3 1.2 fusion.20
  32.6 10.4 %all_to_all.46 = f32[16,8,512]{2,1,0:T(8,128)S(1)} all-to-all(f32[16,8,512]{2,1,0:T(8,128)S(1)} %bitcast.40), channel_id=1, replica_groups=mesh['row'=16,'col'=16] {'row'}, dimensions={0} | all-to-all | bytes 524288 | tf_op jit(solution)/shard_map/all_to_all | solution.py:29
  43.0 10.6 %all_to_all.47 = f32[16,8,512]{2,1,0:T(8,128)S(1)} all-to-all(f32[16,8,512]{2,1,0:T(8,128)S(1)} %broadcast_in_dim.13), channel_id=1, replica_groups=mesh['row'=16,'col'=16] {'row'}, dimensions={0} | all-to-all | bytes 524288 | tf_op jit(solution)/shard_map/all_to_all | solution.py:29
  53.6 0.2 fusion.11
  53.8 5.7 %fusion.2 = f32[16,512]{1,0:T(8,128)S(1)} fusion(bf16[512,8192]{1,0:T(8,128)(2,1)} %param.4, bf16[8,8192]{1,0:T(8,128)(2,1)S(1)} %get-tuple-element.9, bf16[8,8192]{1,0:T(8,128)(2,1)S(1)} %get-tuple-element.8), kind=kOutput, calls=%fused_computation.10 | convolution fusion | flops 134742016 | bytes 8683520 | tf_op jit(solution)/shard_map/dot_general | solution.py:165
  59.5 0.1 reduce-precision_convert_fusion.2
  59.6 4.6 %fusion.24 = f32[16,8192]{1,0:T(8,128)S(1)} fusion(bf16[512,8192]{1,0:T(8,128)(2,1)} %param.4, bf16[8,512]{1,0:T(8,128)(2,1)S(1)} %fusion.13, bf16[8,512]{1,0:T(8,128)(2,1)S(1)} %get-tuple-element.4), kind=kOutput, calls=%fused_computation.41 | convolution fusion | flops 134250496 | bytes 8929280 | tf_op jit(solution)/shard_map/dot_general | solution.py:171
  64.2 10.6 %all_to_all.48 = f32[16,8,512]{2,1,0:T(8,128)S(1)} all-to-all(f32[16,8,512]{2,1,0:T(8,128)S(1)} %bitcast.41), channel_id=1, replica_groups=mesh['row'=16,'col'=16] {'row'}, dimensions={0} | all-to-all | bytes 524288 | tf_op jit(solution)/shard_map/all_to_all | solution.py:29
  74.9 10.6 %all_to_all.49 = f32[16,8,512]{2,1,0:T(8,128)S(1)} all-to-all(f32[16,8,512]{2,1,0:T(8,128)S(1)} %broadcast_in_dim.14), channel_id=1, replica_groups=mesh['row'=16,'col'=16] {'row'}, dimensions={0} | all-to-all | bytes 524288 | tf_op jit(solution)/shard_map/all_to_all | solution.py:29
  85.6 5.6 %fusion.6 = f32[16,512]{1,0:T(8,128)S(1)} fusion(bf16[512,8192]{1,0:T(8,128)(2,1)} %param.4, bf16[8,8192]{1,0:T(8,128)(2,1)S(1)} %get-tuple-element.7, bf16[8,8192]{1,0:T(8,128)(2,1)S(1)} %get-tuple-element.6), kind=kOutput, calls=%fused_computation.14 | convolution fusion | flops 134742016 | bytes 8683520 | tf_op jit(solution)/shard_map/dot_general | solution.py:165
  91.2 0.1 broadcast_in_dim.15
  91.3 0.1 broadcast_in_dim.16
  91.4 32.5 %all_to_all.50 = f32[16,8,1664]{2,1,0:T(8,128)} all-to-all(f32[16,8,1664]{2,1,0:T(8,128)S(1)} %broadcast_in_dim.16), channel_id=1, replica_groups=mesh['row'=16,'col'=16] {'col'}, dimensions={0} | all-to-all | bytes 1703936 | tf_op jit(solution)/shard_map/all_to_all | solution.py:29
  123.9 2.8 %shard_map.59 = f32[512,128]{1,0:T(8,128)} custom-call(f32[128,1664]{1,0:T(8,128)} %bitcast.35), custom_call_target="tpu_custom_call" | custom-call | tf_op jit(solution)/shard_map/pallas_call | solution.py:60
  126.8 13.4 %all_to_all.51 = f32[16,32,128]{2,1,0:T(8,128)S(1)} all-to-all(f32[16,32,128]{2,1,0:T(8,128)} %bitcast.42), channel_id=1, replica_groups=mesh['row'=16,'col'=16] {'row'}, dimensions={0} | all-to-all | bytes 524288 | tf_op jit(solution)/shard_map/all_to_all | solution.py:29
  140.3 11.3 %all_to_all.52 = f32[16,32,128]{2,1,0:T(8,128)} all-to-all(f32[16,32,128]{2,1,0:T(8,128)S(1)} %broadcast_in_dim.17), channel_id=1, replica_groups=mesh['row'=16,'col'=16] {'row'}, dimensions={0} | all-to-all | bytes 524288 | tf_op jit(solution)/shard_map/all_to_all | solution.py:29
  151.6 12.7 %shard_map.60 = (f32[512,128]{1,0:T(8,128)}, f32[512,128]{1,0:T(8,128)}) custom-call(f32[128,1664]{1,0:T(8,128)} %bitcast.36, f32[512,128]{1,0:T(8,128)} %bitcast.39), custom_call_target="tpu_custom_call" | custom-call | tf_op jit(solution)/shard_map/pallas_call | solution.py:148
  (15 shorter events, 0.3 us)
Async XLA Ops:
  0.6 1.0 copy-start
  15.3 10.2 %all-to-all-start.1 = ((bf16[16,8,512]{2,1,0:T(8,128)(2,1)}), bf16[16,8,512]{2,1,0:T(8,128)(2,1)S(1)}, u32[]{:S(2)}, u32[]{:S(2)}) async-start(bf16[16,8,512]{2,1,0:T(8,128)(2,1)} %broadcast_in_dim.12), calls=%async_computation.1 | async-start | bytes 262144 | tf_op jit(solution)/shard_map/all_to_all | solution.py:29
  25.5 5.8 %copy-start.1 = (bf16[512,8192]{1,0:T(8,128)(2,1)S(1)}, bf16[512,8192]{1,0:T(8,128)(2,1)}, u32[]{:S(2)}) copy-start(bf16[512,8192]{1,0:T(8,128)(2,1)} %param.4) | copy-start | bytes 25165828

commit v3 on v2

v3 whole, which is shorter than its diff:
```python
import functools

import jax
import jax.numpy as jnp
from jax import lax
from jax.experimental import pallas as pl
from jax.experimental.pallas import tpu as pltpu
from jax.sharding import PartitionSpec as P

damping = 0.5


def full(left, right, dims=((1,), (0,))):
    return lax.dot_general(
        left,
        right,
        (dims, ((), ())),
        precision=lax.Precision.HIGHEST,
        preferred_element_type=jnp.float32,
    )


def two_terms(value):
    high = value.astype(jnp.bfloat16).astype(jnp.float32)
    return jnp.concatenate([high, value - high]).astype(jnp.bfloat16)


def both_terms(product):
    half = product.shape[0] // 2
    return product[:half] + product[half:]


def bf16_dot(left, right, right_dim):
    return lax.dot_general(
        left, right, (((1,), (right_dim,)), ((), ())), preferred_element_type=jnp.float32
    )


def swap(pieces, axis):
    return lax.all_to_all(pieces, axis, 0, 0, tiled=True)


def spread(piece, axis, size):
    return swap(jnp.broadcast_to(piece[None], (size,) + piece.shape), axis)


def inverse_spd(mat, eye, inv_ref, left_ref):
    on_diag = mat * eye
    across = lax.rsqrt(jnp.sum(on_diag, axis=0, keepdims=True))
    down = lax.rsqrt(jnp.sum(on_diag, axis=1, keepdims=True))
    unit = mat * across * down
    reach = jnp.sum(jnp.abs(unit), axis=1, keepdims=True)
    share = 1.0 / jnp.max(reach, axis=0, keepdims=True)
    left = eye - share * unit
    inv = share * (eye + left)
    left = full(left, left)
    for _ in range(4):
        inv, left = inv + full(inv, left), full(left, left)
    inv_ref[...] = inv
    left_ref[...] = left

    def open_still(state):
        count, size = state
        return jnp.logical_and(count < 40, size > 1e-5)

    def again(state):
        inv, left = inv_ref[...], left_ref[...]
        inv_ref[...] = inv + full(inv, left)
        left = full(left, left)
        left_ref[...] = left
        return state[0] + 1, jnp.sum(left * left)

    lax.while_loop(open_still, again, (0, jnp.sum(left * left)))
    inv = inv_ref[...]
    inv = inv + full(inv, left_ref[...])
    return inv * across * down


def solve_with(mat, inv, right):
    first = full(inv, right)
    return first + full(inv, right - full(mat, first))


def pick_kernel(cols_n, ids_ref, seeds_ref, bank_ref, picked_ref, scale_ref):
    parts, mine, width = picked_ref.shape
    bank_rows = bank_ref.shape[0]
    my_row = lax.axis_index("row")
    my_col = lax.axis_index("col")
    query = lax.broadcasted_iota(jnp.int32, (mine, bank_rows), 0)
    held = lax.broadcasted_iota(jnp.int32, (mine, bank_rows), 1)
    chosen = jnp.zeros((mine, bank_rows), jnp.bool_)
    for q in range(mine):
        local = ids_ref[my_col * mine + q] - my_row * bank_rows
        chosen = jnp.logical_or(chosen, jnp.logical_and(query == q, held == local))
    selector = jnp.where(chosen, 1.0, 0.0).astype(jnp.bfloat16)
    for k in range(parts):
        picked = bf16_dot(selector, bank_ref[:, k * width : (k + 1) * width], 0)
        picked_ref[k] = picked.astype(jnp.bfloat16)
    lanes = seeds_ref.shape[1]
    groups = scale_ref.shape[1] // lanes
    for k in range(groups):
        seeds = seeds_ref[pl.ds(my_row * groups + k, 1), :]
        scale_ref[:, k * lanes : (k + 1) * lanes] = jnp.exp2(seeds.astype(jnp.float32) / 4.0)


def sum_kernel(parts_ref, out_ref):
    total = parts_ref[0].astype(jnp.float32)
    for k in range(1, parts_ref.shape[0]):
        total += parts_ref[k].astype(jnp.float32)
    for k in range(out_ref.shape[0]):
        out_ref[k] = total.astype(out_ref.dtype)


def late_kernel(parts_ref, image_ref, out_ref):
    total = parts_ref[0]
    for k in range(1, parts_ref.shape[0]):
        total += parts_ref[k]
    late = jnp.concatenate([image_ref[...], total], axis=1)
    for k in range(out_ref.shape[0]):
        out_ref[k] = late


def partial_back(value, grads_ref, part_ref):
    terms = two_terms(value)
    parts, _, width = part_ref.shape
    for k in range(parts):
        product = bf16_dot(terms, grads_ref[:, k * width : (k + 1) * width], 0)
        part_ref[k] = both_terms(product)


def base_kernel(chosen_ref, scale_ref, grads_ref, base_ref, part_ref):
    parts, _, width = chosen_ref.shape
    total = jnp.zeros(base_ref.shape, jnp.float32)
    for k in range(parts):
        total += bf16_dot(chosen_ref[k], grads_ref[:, k * width : (k + 1) * width], 1)
    scale = scale_ref[...]
    base = scale * total
    base_ref[...] = base
    partial_back(scale * base, grads_ref, part_ref)


def project(back_ref, grads_ref):
    parts, lead, width = back_ref.shape
    total = jnp.zeros((2 * lead, grads_ref.shape[0]), jnp.float32)
    for k in range(parts):
        total += bf16_dot(two_terms(back_ref[k]), grads_ref[:, k * width : (k + 1) * width], 1)
    return both_terms(total)


def other_kernel(back_ref, chosen_ref, base_ref, scale_ref, grads_ref, message_ref, part_ref):
    parts, lead, width = back_ref.shape
    rows = base_ref.shape[1]
    square = jnp.zeros((lead, width), jnp.float32)
    curve = jnp.zeros((lead, width), jnp.float32)
    for k in range(parts):
        back = back_ref[k]
        square += chosen_ref[k].astype(jnp.float32) * back
        curve += back * back
    square = jnp.sum(square, axis=1, keepdims=True)
    curve = jnp.sum(curve, axis=1, keepdims=True)
    step = square / (curve + damping * square)
    base = base_ref[...]
    scale = scale_ref[...]
    other = base - step * (scale * project(back_ref, grads_ref) + damping * base)
    message_ref[:, :rows] = base
    message_ref[:, rows : 2 * rows] = other
    message_ref[:, 2 * rows :] = jnp.broadcast_to(step, (lead, message_ref.shape[1] - 2 * rows))
    partial_back(scale * other, grads_ref, part_ref)


def image_kernel(back_ref, message_ref, held_ref, scale_ref, grads_ref, image_ref, moments_ref):
    rows = image_ref.shape[1]
    queries = held_ref.shape[0]
    own_base = message_ref[:, :rows]
    own_other = message_ref[:, rows : 2 * rows]
    image = scale_ref[...] * project(back_ref, grads_ref) + damping * own_other
    image_ref[...] = image
    base = held_ref[:, :rows]
    other = held_ref[:, rows : 2 * rows]
    last = ((1,), (1,))
    moments_ref[:, :queries] = full(own_base, base, last)
    moments_ref[:, queries : 2 * queries] = full(own_other, base, last)
    moments_ref[:, 2 * queries : 3 * queries] = full(own_other, other, last)
    moments_ref[:, 3 * queries :] = full(image, other, last)


def finish_kernel(rows, held_ref, late_ref, solution_ref, residual_ref, inv_ref, left_ref):
    queries = held_ref.shape[0]
    bb = late_ref[:, rows : rows + queries]
    tb = late_ref[:, rows + queries : rows + 2 * queries]
    tt = late_ref[:, rows + 2 * queries : rows + 3 * queries]
    tat = late_ref[:, rows + 3 * queries :]
    per_step = 1.0 / held_ref[:, 2 * rows :]
    shape = (queries, queries)
    row_id = lax.broadcasted_iota(jnp.int32, shape, 0)
    eye = jnp.where(row_id == lax.broadcasted_iota(jnp.int32, shape, 1), 1.0, 0.0)

    bab = per_step * (bb - tb)
    bat = per_step * (tb.T - tt)
    tab = bat.T
    inv = inverse_spd(bab, eye, inv_ref, left_ref)
    alpha = solve_with(bab, inv, bb)
    second = per_step * alpha
    second_t = second.T
    first = eye - second
    fresh = full(second_t, tb - full(tab, alpha))
    mixed = -solve_with(bab, inv, full(bat, second))
    curv = full(second_t, full(tab, mixed) + full(tat, second))
    curv = 0.5 * (curv + curv.T)
    inv = inverse_spd(curv, eye, inv_ref, left_ref)
    alpha_next = solve_with(curv, inv, fresh)
    gain = full(mixed, alpha_next)
    gain_other = full(second, alpha_next)
    shift = per_step * gain

    base = held_ref[:, :rows].T
    other = held_ref[:, rows : 2 * rows].T
    image = late_ref[:, :rows].T
    solution_ref[...] = full(base, alpha + gain) + full(other, gain_other)
    residual_ref[...] = full(base, first - shift) + full(other, second + shift) - full(image, gain_other)


def call(kernel, shapes, *args, scratch=(), first=pltpu.VMEM, dtype=jnp.float32, limit=8):
    shapes = [(shape, dtype if k == 0 else jnp.float32) for k, shape in enumerate(shapes)]
    spaces = [first] + [pltpu.VMEM] * (len(args) - 1)
    outs = pl.pallas_call(
        kernel,
        out_shape=tuple(jax.ShapeDtypeStruct(*shape) for shape in shapes),
        in_specs=[pl.BlockSpec(memory_space=space) for space in spaces],
        out_specs=tuple(pl.BlockSpec(memory_space=pltpu.VMEM) for _ in shapes),
        scratch_shapes=scratch,
        compiler_params=pltpu.CompilerParams(vmem_limit_bytes=limit * 2**20),
    )(*args)
    return outs if len(outs) > 1 else outs[0]


def on_device(rows_n, cols_n, grads, seeds, bank, query_ids):
    rows, depth = grads.shape
    queries = query_ids.shape[0]
    mine = queries // cols_n
    lanes = 128
    pieces = (rows_n, mine, depth // rows_n)

    def reduce_row(part):
        total = call(sum_kernel, [part.shape], swap(part, "row"), dtype=part.dtype)
        return swap(total, "row")

    picked, scale = call(
        functools.partial(pick_kernel, cols_n),
        [pieces, (1, rows)],
        query_ids,
        seeds.reshape(-1, lanes),
        bank,
        first=pltpu.SMEM,
        dtype=jnp.bfloat16,
    )
    chosen = reduce_row(picked)
    base, part = call(base_kernel, [(mine, rows), pieces], chosen, scale, grads)
    back = reduce_row(part)
    wide = 2 * rows + lanes
    message, part = call(other_kernel, [(mine, wide), pieces], back, chosen, base, scale, grads)
    held = spread(message, "col", cols_n).reshape(queries, wide)
    back = reduce_row(part)
    image, moments = call(
        image_kernel, [(mine, rows), (mine, 4 * queries)], back, message, held, scale, grads
    )
    late = (cols_n, mine, rows + 4 * queries)
    late = swap(call(late_kernel, [late], spread(moments, "row", rows_n), image), "col")
    square = pltpu.VMEM((queries, queries), jnp.float32)
    return call(
        functools.partial(finish_kernel, rows),
        [(rows, queries), (rows, queries)],
        held,
        late.reshape(queries, rows + 4 * queries),
        scratch=[square, square],
    )


def solution(mesh):
    placed = (P("row", None), P(), P("row", None), P())

    def body(*args):
        return on_device(mesh.shape["row"], mesh.shape["col"], *args)

    return jax.shard_map(
        body,
        mesh=mesh,
        in_specs=placed,
        out_specs=(P("row", None), P("row", None)),
        check_vma=False,
    )
```

time: 165 us -> 154 us (0.933)
  matrix products: 23.1 us -> 0 us
  blocking collectives: 112 us -> 124 us
  Pallas kernels: 15.5 us -> 22.5 us
  waiting for transfers between devices: 5.44 us -> 0 us
  local copies, waits for them, and re-layouts: 1.05 us -> 5.82 us
  starting transfers between devices: 3.96 us -> 0 us
  other arithmetic: 2.1 us -> 0 us
    dot_general x6 -> x0, matrix products: 23.1 us -> none  [the longest x2 11.3 us: project(): lax.dot_general(two_terms(value), grads, (((1,), (1,)), ((), ())), prefer...]
    all_to_all x8 -> x9, blocking collectives: 112 us -> 124 us  [swap(): return lax.all_to_all(pieces, axis, 0, 0, tiled=True)]
    pallas_call x2 -> x9, Pallas kernels: 15.5 us -> 22.5 us  [call(): pl.pallas_call(kernel, out_shape=tuple((jax.ShapeDtypeStruct(*shape) for...]
    unnamed x4 -> x10, local copies, waits for them, and re-layouts: 0.2 us -> 5.74 us
    all_to_all x1 -> x0, waiting for transfers between devices: 5.44 us -> none  [swap(): return lax.all_to_all(pieces, axis, 0, 0, tiled=True)]
    all_to_all x1 -> x0, starting transfers between devices: 3.96 us -> none  [swap(): return lax.all_to_all(pieces, axis, 0, 0, tiled=True)]
  transfers between devices with their start and end apart: 1 -> 0, of which waited for: 1 -> 0; matrix products, arithmetic and copies ran while one was open for 0% -> 0% of each run, Pallas kernels for 0% -> 0%
where the time goes in v3:
time: 154 us; the launch traced here: 153 us
  blocking collectives  124 us (81%)
  Pallas kernels  22.5 us (15%)
  local copies, waits for them, and re-layouts  5.82 us (4%)
    all_to_all x9, blocking collectives, swap(): return lax.all_to_all(pieces, axis, 0, 0, tiled=True)  124 us
    pallas_call x9, Pallas kernels, call(): pl.pallas_call(kernel, out_shape=tuple((jax.ShapeDtypeStruct(*shape) for...  22.5 us
    unnamed x10, local copies, waits for them, and re-layouts  5.74 us

profile of v3, /device:TPU:1, one launch (start us, length us, event | category | flops | bytes accessed | tf_op | source)
XLA Modules:
  0.0 152.6 jit_solution(3370886265886125209)
XLA Ops:
  0.6 0.0 copy-start.2
  0.6 0.9 copy-done.2
  1.6 0.0 copy-start.3
  1.6 0.8 copy-done.3
  2.3 0.0 copy-start.4
  2.3 0.7 copy-done.4
  3.0 0.8 shard_map.59
  3.8 12.8 %all_to_all.45.parts_ref = bf16[16,8,512]{2,1,0:T(8,128)(2,1)S(1)} all-to-all(bf16[16,8,512]{2,1,0:T(8,128)(2,1)S(1)} %get-tuple-element.10), channel_id=1, replica_groups=mesh['row'=16,'col'=16] {'row'}, dimensions={0} | all-to-all | bytes 262144 | tf_op jit(solution)/shard_map/all_to_all | solution.py:40
  16.6 9.3 %all_to_all.46.chosen_ref = bf16[16,8,512]{2,1,0:T(8,128)(2,1)S(1)} all-to-all(bf16[16,8,512]{2,1,0:T(8,128)(2,1)S(1)} %shard_map.60), channel_id=1, replica_groups=mesh['row'=16,'col'=16] {'row'}, dimensions={0} | all-to-all | bytes 262144 | tf_op jit(solution)/shard_map/all_to_all | solution.py:40
  25.9 0.0 copy-start
  25.9 3.4 %copy-done = bf16[512,8192]{1,0:T(8,128)(2,1)S(1)} copy-done((bf16[512,8192]{1,0:T(8,128)(2,1)S(1)}, bf16[512,8192]{1,0:T(8,128)(2,1)}, u32[]{:S(2)}) %copy-start) | copy-done | bytes 8388632
  29.2 0.0 copy-start.1
  29.2 3.4 %shard_map.61 = (f32[8,512]{1,0:T(8,128)S(1)}, f32[16,8,512]{2,1,0:T(8,128)S(1)}) custom-call(bf16[16,8,512]{2,1,0:T(8,128)(2,1)S(1)} %all_to_all.46.chosen_ref, f32[1,512]{1,0:T(1,128)S(1)} %get-tuple-element.11.scale_ref, bf16[512,8192]{1,0:T(8,128)(2,1)S(1)} %copy-done), custom_call_target="tpu_custom_call" | custom-call | tf_op jit(solution)/shard_map/pallas_call | solution.py:226
  32.7 10.4 %all_to_all.47.parts_ref = f32[16,8,512]{2,1,0:T(8,128)S(1)} all-to-all(f32[16,8,512]{2,1,0:T(8,128)S(1)} %get-tuple-element.12), channel_id=1, replica_groups=mesh['row'=16,'col'=16] {'row'}, dimensions={0} | all-to-all | bytes 524288 | tf_op jit(solution)/shard_map/all_to_all | solution.py:40
  43.1 10.6 %all_to_all.48.back_ref = f32[16,8,512]{2,1,0:T(8,128)S(1)} all-to-all(f32[16,8,512]{2,1,0:T(8,128)S(1)} %shard_map.62), channel_id=1, replica_groups=mesh['row'=16,'col'=16] {'row'}, dimensions={0} | all-to-all | bytes 524288 | tf_op jit(solution)/shard_map/all_to_all | solution.py:40
  53.7 0.0 copy-done.1
  53.7 3.4 %shard_map.63 = (f32[8,1152]{1,0:T(8,128)S(1)}, f32[16,8,512]{2,1,0:T(8,128)S(1)}) custom-call(f32[16,8,512]{2,1,0:T(8,128)S(1)} %all_to_all.48.back_ref, bf16[16,8,512]{2,1,0:T(8,128)(2,1)S(1)} %all_to_all.46.chosen_ref, f32[8,512]{1,0:T(8,128)S(1)} %get-tuple-element.13.base_ref, f32[1,512]{1,0:T(1,128)S(1)} %get-tuple-element.11.scale_ref, ...), custom_call_target="tpu_custom_call" | custom-call | tf_op jit(solution)/shard_map/pallas_call | solution.py:226
  57.1 10.6 %all_to_all.49.parts_ref = f32[16,8,512]{2,1,0:T(8,128)S(1)} all-to-all(f32[16,8,512]{2,1,0:T(8,128)S(1)} %get-tuple-element.15), channel_id=1, replica_groups=mesh['row'=16,'col'=16] {'row'}, dimensions={0} | all-to-all | bytes 524288 | tf_op jit(solution)/shard_map/all_to_all | solution.py:40
  67.8 10.6 %all_to_all.50.back_ref = f32[16,8,512]{2,1,0:T(8,128)S(1)} all-to-all(f32[16,8,512]{2,1,0:T(8,128)S(1)} %shard_map.64), channel_id=1, replica_groups=mesh['row'=16,'col'=16] {'row'}, dimensions={0} | all-to-all | bytes 524288 | tf_op jit(solution)/shard_map/all_to_all | solution.py:40
  78.5 28.5 %all_to_all.51 = f32[16,8,1152]{2,1,0:T(8,128)S(1)} all-to-all(f32[16,8,1152]{2,1,0:T(8,128)S(1)} %broadcast_in_dim.4), channel_id=1, replica_groups=mesh['row'=16,'col'=16] {'col'}, dimensions={0} | all-to-all | bytes 1179648 | tf_op jit(solution)/shard_map/all_to_all | solution.py:40
  106.9 3.1 %shard_map.65 = (f32[8,512]{1,0:T(8,128)S(1)}, f32[8,512]{1,0:T(8,128)S(1)}) custom-call(f32[16,8,512]{2,1,0:T(8,128)S(1)} %all_to_all.50.back_ref, f32[8,1152]{1,0:T(8,128)S(1)} %get-tuple-element.14.message_ref, f32[128,1152]{1,0:T(8,128)S(1)} %bitcast.3, f32[1,512]{1,0:T(1,128)S(1)} %get-tuple-element.11.scale_ref, bf16[512,8192]{1,0:T(8,128)(2,1)S(1)} %copy-done.1), custom_call_target="tpu_custom_call" | custom-call | tf_op jit(solution)/shard_map/pallas_call | solution.py:226
  110.1 13.0 %all_to_all.52.parts_ref = f32[16,8,512]{2,1,0:T(8,128)S(1)} all-to-all(f32[16,8,512]{2,1,0:T(8,128)S(1)} %broadcast_in_dim.5), channel_id=1, replica_groups=mesh['row'=16,'col'=16] {'row'}, dimensions={0} | all-to-all | bytes 524288 | tf_op jit(solution)/shard_map/all_to_all | solution.py:40
  123.1 17.9 %all_to_all.53 = f32[16,8,1024]{2,1,0:T(8,128)S(1)} all-to-all(f32[16,8,1024]{2,1,0:T(8,128)S(1)} %shard_map.66), channel_id=1, replica_groups=mesh['row'=16,'col'=16] {'col'}, dimensions={0} | all-to-all | bytes 1048576 | tf_op jit(solution)/shard_map/all_to_all | solution.py:40
  141.0 11.6 %shard_map.67 = (f32[512,128]{1,0:T(8,128)}, f32[512,128]{1,0:T(8,128)}) custom-call(f32[128,1152]{1,0:T(8,128)S(1)} %bitcast.4, f32[128,1024]{1,0:T(8,128)S(1)} %bitcast.5), custom_call_target="tpu_custom_call" | custom-call | tf_op jit(solution)/shard_map/pallas_call | solution.py:226
  (6 shorter events, 0.2 us)
Async XLA Ops:
  0.6 1.0 copy-start.2
  1.6 0.8 copy-start.3
  2.3 0.7 copy-start.4
  25.9 3.4 %copy-start = (bf16[512,8192]{1,0:T(8,128)(2,1)S(1)}, bf16[512,8192]{1,0:T(8,128)(2,1)}, u32[]{:S(2)}) copy-start(bf16[512,8192]{1,0:T(8,128)(2,1)} %grads_ref.5) | copy-start | bytes 25165828
  29.2 24.5 %copy-start.1 = (bf16[512,8192]{1,0:T(8,128)(2,1)S(1)}, bf16[512,8192]{1,0:T(8,128)(2,1)}, u32[]{:S(2)}) copy-start(bf16[512,8192]{1,0:T(8,128)(2,1)} %grads_ref.5) | copy-start | bytes 25165828

commit v4 on v3

--- a/solution.py
+++ b/solution.py
@@ -81,7 +81,17 @@
     return first + full(inv, right - full(mat, first))
 
 
-def pick_kernel(cols_n, ids_ref, seeds_ref, bank_ref, picked_ref, scale_ref):
+def pick_kernel(
+    cols_n, ids_hbm, seeds_hbm, bank_hbm, picked_ref, scale_ref, ids_ref, seeds_ref, bank_ref, sems
+):
+    copies = [
+        pltpu.make_async_copy(source, target, sems.at[k])
+        for k, (source, target) in enumerate(
+            [(ids_hbm, ids_ref), (bank_hbm, bank_ref), (seeds_hbm, seeds_ref)]
+        )
+    ]
+    for copy in copies:
+        copy.start()
     parts, mine, width = picked_ref.shape
     bank_rows = bank_ref.shape[0]
     my_row = lax.axis_index("row")
@@ -89,15 +99,18 @@
     query = lax.broadcasted_iota(jnp.int32, (mine, bank_rows), 0)
     held = lax.broadcasted_iota(jnp.int32, (mine, bank_rows), 1)
     chosen = jnp.zeros((mine, bank_rows), jnp.bool_)
+    copies[0].wait()
     for q in range(mine):
         local = ids_ref[my_col * mine + q] - my_row * bank_rows
         chosen = jnp.logical_or(chosen, jnp.logical_and(query == q, held == local))
     selector = jnp.where(chosen, 1.0, 0.0).astype(jnp.bfloat16)
+    copies[1].wait()
     for k in range(parts):
         picked = bf16_dot(selector, bank_ref[:, k * width : (k + 1) * width], 0)
         picked_ref[k] = picked.astype(jnp.bfloat16)
     lanes = seeds_ref.shape[1]
     groups = scale_ref.shape[1] // lanes
+    copies[2].wait()
     for k in range(groups):
         seeds = seeds_ref[pl.ds(my_row * groups + k, 1), :]
         scale_ref[:, k * lanes : (k + 1) * lanes] = jnp.exp2(seeds.astype(jnp.float32) / 4.0)
@@ -128,10 +141,16 @@
         part_ref[k] = both_terms(product)
 
 
-def base_kernel(chosen_ref, scale_ref, grads_ref, base_ref, part_ref):
-    parts, _, width = chosen_ref.shape
+def base_kernel(chosen_ref, scale_ref, grads_hbm, base_ref, part_ref, grads_ref, sems):
+    parts, lead, width = chosen_ref.shape
+    copies = []
+    for k in range(parts):
+        block = (slice(None), pl.ds(k * width, width))
+        copies.append(pltpu.make_async_copy(grads_hbm.at[block], grads_ref.at[block], sems.at[k]))
+        copies[k].start()
     total = jnp.zeros(base_ref.shape, jnp.float32)
     for k in range(parts):
+        copies[k].wait()
         total += bf16_dot(chosen_ref[k], grads_ref[:, k * width : (k + 1) * width], 1)
     scale = scale_ref[...]
     base = scale * total
@@ -220,18 +239,27 @@
     residual_ref[...] = full(base, first - shift) + full(other, second + shift) - full(image, gain_other)
 
 
-def call(kernel, shapes, *args, scratch=(), first=pltpu.VMEM, dtype=jnp.float32, limit=8):
-    shapes = [(shape, dtype if k == 0 else jnp.float32) for k, shape in enumerate(shapes)]
-    spaces = [first] + [pltpu.VMEM] * (len(args) - 1)
+def call(kernel, shapes, *args, scratch=(), dtypes=(jnp.float32, jnp.float32), limit=8):
     outs = pl.pallas_call(
         kernel,
-        out_shape=tuple(jax.ShapeDtypeStruct(*shape) for shape in shapes),
-        in_specs=[pl.BlockSpec(memory_space=space) for space in spaces],
+        out_shape=tuple(jax.ShapeDtypeStruct(*shape) for shape in zip(shapes, dtypes)),
+        in_specs=[pl.BlockSpec(memory_space=pltpu.VMEM if near else pl.ANY) for near, _ in map(place, args)],
         out_specs=tuple(pl.BlockSpec(memory_space=pltpu.VMEM) for _ in shapes),
         scratch_shapes=scratch,
         compiler_params=pltpu.CompilerParams(vmem_limit_bytes=limit * 2**20),
-    )(*args)
+    )(*(value for _, value in map(place, args)))
     return outs if len(outs) > 1 else outs[0]
+
+
+class Far:
+    def __init__(self, value):
+        self.value = value
+
+
+def place(arg):
+    if isinstance(arg, Far):
+        return False, pltpu.with_memory_space_constraint(arg.value, pltpu.MemorySpace.HBM)
+    return True, arg
 
 
 def on_device(rows_n, cols_n, grads, seeds, bank, query_ids):
@@ -242,20 +270,34 @@
     pieces = (rows_n, mine, depth // rows_n)
 
     def reduce_row(part):
-        total = call(sum_kernel, [part.shape], swap(part, "row"), dtype=part.dtype)
+        total = call(sum_kernel, [part.shape], swap(part, "row"), dtypes=[part.dtype])
         return swap(total, "row")
 
+    seeds = seeds.reshape(-1, lanes)
     picked, scale = call(
         functools.partial(pick_kernel, cols_n),
         [pieces, (1, rows)],
-        query_ids,
-        seeds.reshape(-1, lanes),
-        bank,
-        first=pltpu.SMEM,
-        dtype=jnp.bfloat16,
+        Far(query_ids),
+        Far(seeds),
+        Far(bank),
+        scratch=[
+            pltpu.SMEM(query_ids.shape, jnp.int32),
+            pltpu.VMEM(seeds.shape, jnp.int32),
+            pltpu.VMEM(bank.shape, bank.dtype),
+            pltpu.SemaphoreType.DMA((3,)),
+        ],
+        dtypes=[bank.dtype, jnp.float32],
     )
     chosen = reduce_row(picked)
-    base, part = call(base_kernel, [(mine, rows), pieces], chosen, scale, grads)
+    base, part, grads = call(
+        base_kernel,
+        [(mine, rows), pieces, grads.shape],
+        chosen,
+        scale,
+        Far(grads),
+        scratch=[pltpu.SemaphoreType.DMA((rows_n,))],
+        dtypes=[jnp.float32, jnp.float32, grads.dtype],
+    )
     back = reduce_row(part)
     wide = 2 * rows + lanes
     message, part = call(other_kernel, [(mine, wide), pieces], back, chosen, base, scale, grads)

time: 154 us -> 150 us (0.974)
  local copies, waits for them, and re-layouts: 5.82 us -> 0.08 us
  Pallas kernels: 22.5 us -> 24.5 us
    unnamed x10 -> x0, local copies, waits for them, and re-layouts: 5.74 us -> none
    pallas_call x9, Pallas kernels: 22.5 us -> 24.5 us  [call(): pl.pallas_call(kernel, out_shape=tuple((jax.ShapeDtypeStruct(*shape) for...]
where the time goes in v4:
time: 150 us; the launch traced here: 149 us
  blocking collectives  124 us (83%)
  Pallas kernels  24.5 us (16%)
    all_to_all x9, blocking collectives, swap(): return lax.all_to_all(pieces, axis, 0, 0, tiled=True)  124 us
    pallas_call x9, Pallas kernels, call(): pl.pallas_call(kernel, out_shape=tuple((jax.ShapeDtypeStruct(*shape) for...  24.5 us

profile of v4, /device:TPU:1, one launch (start us, length us, event | category | flops | bytes accessed | tf_op | source)
XLA Modules:
  0.0 148.9 jit_solution(17597272134097123913)
XLA Ops:
  0.6 1.2 shard_map.59
  1.8 12.8 %all_to_all.45.parts_ref = bf16[16,8,512]{2,1,0:T(8,128)(2,1)S(1)} all-to-all(bf16[16,8,512]{2,1,0:T(8,128)(2,1)S(1)} %get-tuple-element.11), channel_id=1, replica_groups=mesh['row'=16,'col'=16] {'row'}, dimensions={0} | all-to-all | bytes 262144 | tf_op jit(solution)/shard_map/all_to_all | solution.py:40
  14.7 9.3 %all_to_all.46.chosen_ref = bf16[16,8,512]{2,1,0:T(8,128)(2,1)S(1)} all-to-all(bf16[16,8,512]{2,1,0:T(8,128)(2,1)S(1)} %shard_map.60), channel_id=1, replica_groups=mesh['row'=16,'col'=16] {'row'}, dimensions={0} | all-to-all | bytes 262144 | tf_op jit(solution)/shard_map/all_to_all | solution.py:40
  23.9 5.0 %shard_map.61 = (f32[8,512]{1,0:T(8,128)S(1)}, f32[16,8,512]{2,1,0:T(8,128)S(1)}, bf16[512,8192]{1,0:T(8,128)(2,1)S(1)}) custom-call(bf16[16,8,512]{2,1,0:T(8,128)(2,1)S(1)} %all_to_all.46.chosen_ref, f32[1,512]{1,0:T(1,128)S(1)} %get-tuple-element.12.scale_ref, bf16[512,8192]{1,0:T(8,128)(2,1)} %grads_hbm.1), custom_call_target="tpu_custom_call" | custom-call | tf_op jit(solution)/shard_map/pallas_call | solution.py:243
  28.9 10.4 %all_to_all.47.parts_ref = f32[16,8,512]{2,1,0:T(8,128)S(1)} all-to-all(f32[16,8,512]{2,1,0:T(8,128)S(1)} %get-tuple-element.13), channel_id=1, replica_groups=mesh['row'=16,'col'=16] {'row'}, dimensions={0} | all-to-all | bytes 524288 | tf_op jit(solution)/shard_map/all_to_all | solution.py:40
  39.3 10.6 %all_to_all.48.back_ref = f32[16,8,512]{2,1,0:T(8,128)S(1)} all-to-all(f32[16,8,512]{2,1,0:T(8,128)S(1)} %shard_map.62), channel_id=1, replica_groups=mesh['row'=16,'col'=16] {'row'}, dimensions={0} | all-to-all | bytes 524288 | tf_op jit(solution)/shard_map/all_to_all | solution.py:40
  50.0 3.4 %shard_map.63 = (f32[8,1152]{1,0:T(8,128)S(1)}, f32[16,8,512]{2,1,0:T(8,128)S(1)}) custom-call(f32[16,8,512]{2,1,0:T(8,128)S(1)} %all_to_all.48.back_ref, bf16[16,8,512]{2,1,0:T(8,128)(2,1)S(1)} %all_to_all.46.chosen_ref, f32[8,512]{1,0:T(8,128)S(1)} %get-tuple-element.14.base_ref, f32[1,512]{1,0:T(1,128)S(1)} %get-tuple-element.12.scale_ref, ...), custom_call_target="tpu_custom_call" | custom-call | tf_op jit(solution)/shard_map/pallas_call | solution.py:243
  53.4 10.6 %all_to_all.49.parts_ref = f32[16,8,512]{2,1,0:T(8,128)S(1)} all-to-all(f32[16,8,512]{2,1,0:T(8,128)S(1)} %get-tuple-element.17), channel_id=1, replica_groups=mesh['row'=16,'col'=16] {'row'}, dimensions={0} | all-to-all | bytes 524288 | tf_op jit(solution)/shard_map/all_to_all | solution.py:40
  64.1 10.6 %all_to_all.50.back_ref = f32[16,8,512]{2,1,0:T(8,128)S(1)} all-to-all(f32[16,8,512]{2,1,0:T(8,128)S(1)} %shard_map.64), channel_id=1, replica_groups=mesh['row'=16,'col'=16] {'row'}, dimensions={0} | all-to-all | bytes 524288 | tf_op jit(solution)/shard_map/all_to_all | solution.py:40
  74.7 28.5 %all_to_all.51 = f32[16,8,1152]{2,1,0:T(8,128)S(1)} all-to-all(f32[16,8,1152]{2,1,0:T(8,128)S(1)} %broadcast_in_dim.4), channel_id=1, replica_groups=mesh['row'=16,'col'=16] {'col'}, dimensions={0} | all-to-all | bytes 1179648 | tf_op jit(solution)/shard_map/all_to_all | solution.py:40
  103.2 3.1 %shard_map.65 = (f32[8,512]{1,0:T(8,128)S(1)}, f32[8,512]{1,0:T(8,128)S(1)}) custom-call(f32[16,8,512]{2,1,0:T(8,128)S(1)} %all_to_all.50.back_ref, f32[8,1152]{1,0:T(8,128)S(1)} %get-tuple-element.16.message_ref, f32[128,1152]{1,0:T(8,128)S(1)} %bitcast.3, f32[1,512]{1,0:T(1,128)S(1)} %get-tuple-element.12.scale_ref, ...), custom_call_target="tpu_custom_call" | custom-call | tf_op jit(solution)/shard_map/pallas_call | solution.py:243
  106.3 13.0 %all_to_all.52.parts_ref = f32[16,8,512]{2,1,0:T(8,128)S(1)} all-to-all(f32[16,8,512]{2,1,0:T(8,128)S(1)} %broadcast_in_dim.5), channel_id=1, replica_groups=mesh['row'=16,'col'=16] {'row'}, dimensions={0} | all-to-all | bytes 524288 | tf_op jit(solution)/shard_map/all_to_all | solution.py:40
  119.4 17.9 %all_to_all.53 = f32[16,8,1024]{2,1,0:T(8,128)S(1)} all-to-all(f32[16,8,1024]{2,1,0:T(8,128)S(1)} %shard_map.66), channel_id=1, replica_groups=mesh['row'=16,'col'=16] {'col'}, dimensions={0} | all-to-all | bytes 1048576 | tf_op jit(solution)/shard_map/all_to_all | solution.py:40
  137.3 11.6 %shard_map.67 = (f32[512,128]{1,0:T(8,128)}, f32[512,128]{1,0:T(8,128)}) custom-call(f32[128,1152]{1,0:T(8,128)S(1)} %bitcast.4, f32[128,1024]{1,0:T(8,128)S(1)} %bitcast.5), custom_call_target="tpu_custom_call" | custom-call | tf_op jit(solution)/shard_map/pallas_call | solution.py:243
  (6 shorter events, 0.2 us)

commit v5 on v4

--- a/solution.py
+++ b/solution.py
@@ -36,6 +36,24 @@
     )
 
 
+def halves(value):
+    high = value.astype(jnp.bfloat16)
+    return high, (value - high.astype(jnp.float32)).astype(jnp.bfloat16)
+
+
+def product(left, right):
+    high, low = halves(right)
+    top = jnp.concatenate([high, low], axis=1)
+    bottom = jnp.concatenate([high, jnp.zeros_like(low)], axis=1)
+    both = jnp.dot(
+        jnp.concatenate(halves(left), axis=1),
+        jnp.concatenate([top, bottom], axis=0),
+        preferred_element_type=jnp.float32,
+    )
+    columns = right.shape[1]
+    return both[:, :columns] + both[:, columns:]
+
+
 def swap(pieces, axis):
     return lax.all_to_all(pieces, axis, 0, 0, tiled=True)
 
@@ -44,7 +62,8 @@
     return swap(jnp.broadcast_to(piece[None], (size,) + piece.shape), axis)
 
 
-def inverse_spd(mat, eye, inv_ref, left_ref):
+def inverse_spd(mat, eye, both_ref):
+    size = mat.shape[0]
     on_diag = mat * eye
     across = lax.rsqrt(jnp.sum(on_diag, axis=0, keepdims=True))
     down = lax.rsqrt(jnp.sum(on_diag, axis=1, keepdims=True))
@@ -53,36 +72,40 @@
     share = 1.0 / jnp.max(reach, axis=0, keepdims=True)
     left = eye - share * unit
     inv = share * (eye + left)
-    left = full(left, left)
+    left = product(left, left)
+
+    def advance(inv, left):
+        both = product(jnp.concatenate([inv, left]), left)
+        return inv + both[:size], both[size:]
+
     for _ in range(4):
-        inv, left = inv + full(inv, left), full(left, left)
-    inv_ref[...] = inv
-    left_ref[...] = left
+        inv, left = advance(inv, left)
+    both_ref[:size] = inv
+    both_ref[size:] = left
 
     def open_still(state):
-        count, size = state
-        return jnp.logical_and(count < 40, size > 1e-5)
+        count, remainder = state
+        return jnp.logical_and(count < 40, remainder > 1e-5)
 
     def again(state):
-        inv, left = inv_ref[...], left_ref[...]
-        inv_ref[...] = inv + full(inv, left)
-        left = full(left, left)
-        left_ref[...] = left
+        inv, left = advance(both_ref[:size], both_ref[size:])
+        both_ref[:size] = inv
+        both_ref[size:] = left
         return state[0] + 1, jnp.sum(left * left)
 
     lax.while_loop(open_still, again, (0, jnp.sum(left * left)))
-    inv = inv_ref[...]
-    inv = inv + full(inv, left_ref[...])
+    inv = both_ref[:size]
+    inv = inv + product(inv, both_ref[size:])
     return inv * across * down
 
 
 def solve_with(mat, inv, right):
-    first = full(inv, right)
-    return first + full(inv, right - full(mat, first))
+    first = product(inv, right)
+    return first + product(inv, right - full(mat, first))
 
 
 def pick_kernel(
-    cols_n, ids_hbm, seeds_hbm, bank_hbm, picked_ref, scale_ref, ids_ref, seeds_ref, bank_ref, sems
+    ids_hbm, seeds_hbm, bank_hbm, picked_ref, scale_ref, ids_ref, seeds_ref, bank_ref, sems
 ):
     copies = [
         pltpu.make_async_copy(source, target, sems.at[k])
@@ -142,7 +165,7 @@
 
 
 def base_kernel(chosen_ref, scale_ref, grads_hbm, base_ref, part_ref, grads_ref, sems):
-    parts, lead, width = chosen_ref.shape
+    parts, _, width = chosen_ref.shape
     copies = []
     for k in range(parts):
         block = (slice(None), pl.ds(k * width, width))
@@ -158,11 +181,12 @@
     partial_back(scale * base, grads_ref, part_ref)
 
 
-def project(back_ref, grads_ref):
-    parts, lead, width = back_ref.shape
+def project(back_ref, grads_ref, width):
+    parts, lead, _ = back_ref.shape
     total = jnp.zeros((2 * lead, grads_ref.shape[0]), jnp.float32)
     for k in range(parts):
-        total += bf16_dot(two_terms(back_ref[k]), grads_ref[:, k * width : (k + 1) * width], 1)
+        terms = two_terms(back_ref[k, :, :width])
+        total += bf16_dot(terms, grads_ref[:, k * width : (k + 1) * width], 1)
     return both_terms(total)
 
 
@@ -180,35 +204,44 @@
     step = square / (curve + damping * square)
     base = base_ref[...]
     scale = scale_ref[...]
-    other = base - step * (scale * project(back_ref, grads_ref) + damping * base)
+    other = base - step * (scale * project(back_ref, grads_ref, width) + damping * base)
     message_ref[:, :rows] = base
     message_ref[:, rows : 2 * rows] = other
     message_ref[:, 2 * rows :] = jnp.broadcast_to(step, (lead, message_ref.shape[1] - 2 * rows))
     partial_back(scale * other, grads_ref, part_ref)
 
 
-def image_kernel(back_ref, message_ref, held_ref, scale_ref, grads_ref, image_ref, moments_ref):
-    rows = image_ref.shape[1]
-    queries = held_ref.shape[0]
-    own_base = message_ref[:, :rows]
-    own_other = message_ref[:, rows : 2 * rows]
-    image = scale_ref[...] * project(back_ref, grads_ref) + damping * own_other
-    image_ref[...] = image
+def join_kernel(part_ref, held_ref, out_ref):
+    parts, lead, width = part_ref.shape
+    rows = (held_ref.shape[1] - 128) // 2
     base = held_ref[:, :rows]
     other = held_ref[:, rows : 2 * rows]
     last = ((1,), (1,))
-    moments_ref[:, :queries] = full(own_base, base, last)
-    moments_ref[:, queries : 2 * queries] = full(own_other, base, last)
-    moments_ref[:, 2 * queries : 3 * queries] = full(own_other, other, last)
-    moments_ref[:, 3 * queries :] = full(image, other, last)
-
-
-def finish_kernel(rows, held_ref, late_ref, solution_ref, residual_ref, inv_ref, left_ref):
+    inner = [full(base, base, last), full(other, base, last), full(other, other, last)]
+    for k in range(parts):
+        out_ref[k, :, :width] = part_ref[k]
+        for n, mat in enumerate(inner):
+            lanes = slice(width + n * mat.shape[1], width + (n + 1) * mat.shape[1])
+            out_ref[k, :, lanes] = mat[k * lead : (k + 1) * lead]
+
+
+def image_kernel(back_ref, message_ref, held_ref, scale_ref, grads_ref, image_ref, inner_ref):
+    rows = image_ref.shape[1]
+    width = grads_ref.shape[1] // back_ref.shape[0]
+    own_other = message_ref[:, rows : 2 * rows]
+    image = scale_ref[...] * project(back_ref, grads_ref, width) + damping * own_other
+    image_ref[...] = image
+    inner_ref[...] = full(image, held_ref[:, rows : 2 * rows], ((1,), (1,)))
+
+
+def first_kernel(width, back_ref, held_ref, solved_ref, terms_ref, both_ref):
     queries = held_ref.shape[0]
-    bb = late_ref[:, rows : rows + queries]
-    tb = late_ref[:, rows + queries : rows + 2 * queries]
-    tt = late_ref[:, rows + 2 * queries : rows + 3 * queries]
-    tat = late_ref[:, rows + 3 * queries :]
+    rows = terms_ref.shape[0]
+    parts = range(back_ref.shape[0])
+    bb, tb, tt = (
+        jnp.concatenate([back_ref[k, :, width + n * queries : width + (n + 1) * queries] for k in parts])
+        for n in range(3)
+    )
     per_step = 1.0 / held_ref[:, 2 * rows :]
     shape = (queries, queries)
     row_id = lax.broadcasted_iota(jnp.int32, shape, 0)
@@ -217,26 +250,55 @@
     bab = per_step * (bb - tb)
     bat = per_step * (tb.T - tt)
     tab = bat.T
-    inv = inverse_spd(bab, eye, inv_ref, left_ref)
+    inv = inverse_spd(bab, eye, both_ref)
     alpha = solve_with(bab, inv, bb)
     second = per_step * alpha
-    second_t = second.T
+    fresh = product(second.T, tb - full(tab, alpha))
+    mixed = -solve_with(bab, inv, product(bat, second))
+    for k, mat in enumerate([alpha, second, fresh, mixed, product(tab, mixed)]):
+        solved_ref[k] = mat
+    for k in range(2):
+        block = held_ref[:, k * rows : (k + 1) * rows].T
+        terms_ref[:, 2 * k * queries : 2 * (k + 1) * queries] = jnp.concatenate(halves(block), axis=1)
+
+
+def finish_kernel(held_ref, solved_ref, terms_ref, late_ref, solution_ref, residual_ref, both_ref):
+    queries = held_ref.shape[0]
+    rows = terms_ref.shape[0]
+    tat = late_ref[:, rows:]
+    per_step = 1.0 / held_ref[:, 2 * rows :]
+    alpha, second, fresh, mixed, lead = (solved_ref[k] for k in range(5))
+    shape = (queries, queries)
+    row_id = lax.broadcasted_iota(jnp.int32, shape, 0)
+    eye = jnp.where(row_id == lax.broadcasted_iota(jnp.int32, shape, 1), 1.0, 0.0)
+    curv = product(second.T, lead + product(tat, second))
+    curv = 0.5 * (curv + curv.T)
+    image = jnp.concatenate(halves(late_ref[:, :rows].T), axis=1)
+    inv = inverse_spd(curv, eye, both_ref)
+    alpha_next = solve_with(curv, inv, fresh)
+    gain = product(jnp.concatenate([mixed, second]), alpha_next)
+    gain, gain_other = gain[:queries], gain[queries:]
+    shift = per_step * gain
+
+    def times(terms, right):
+        high, low = halves(right)
+        both = jnp.dot(
+            terms,
+            jnp.concatenate(
+                [
+                    jnp.concatenate([high, low], axis=1),
+                    jnp.concatenate([high, jnp.zeros_like(low)], axis=1),
+                ]
+            ),
+            preferred_element_type=jnp.float32,
+        )
+        return both[:, : right.shape[1]] + both[:, right.shape[1] :]
+
     first = eye - second
-    fresh = full(second_t, tb - full(tab, alpha))
-    mixed = -solve_with(bab, inv, full(bat, second))
-    curv = full(second_t, full(tab, mixed) + full(tat, second))
-    curv = 0.5 * (curv + curv.T)
-    inv = inverse_spd(curv, eye, inv_ref, left_ref)
-    alpha_next = solve_with(curv, inv, fresh)
-    gain = full(mixed, alpha_next)
-    gain_other = full(second, alpha_next)
-    shift = per_step * gain
-
-    base = held_ref[:, :rows].T
-    other = held_ref[:, rows : 2 * rows].T
-    image = late_ref[:, :rows].T
-    solution_ref[...] = full(base, alpha + gain) + full(other, gain_other)
-    residual_ref[...] = full(base, first - shift) + full(other, second + shift) - full(image, gain_other)
+    out = times(terms_ref[:, : 2 * queries], jnp.concatenate([alpha + gain, first - shift], axis=1))
+    out += times(terms_ref[:, 2 * queries :], jnp.concatenate([gain_other, second + shift], axis=1))
+    solution_ref[...] = out[:, :queries]
+    residual_ref[...] = out[:, queries:] - times(image, gain_other)
 
 
 def call(kernel, shapes, *args, scratch=(), dtypes=(jnp.float32, jnp.float32), limit=8):
@@ -275,7 +337,7 @@
 
     seeds = seeds.reshape(-1, lanes)
     picked, scale = call(
-        functools.partial(pick_kernel, cols_n),
+        pick_kernel,
         [pieces, (1, rows)],
         Far(query_ids),
         Far(seeds),
@@ -302,19 +364,32 @@
     wide = 2 * rows + lanes
     message, part = call(other_kernel, [(mine, wide), pieces], back, chosen, base, scale, grads)
     held = spread(message, "col", cols_n).reshape(queries, wide)
-    back = reduce_row(part)
-    image, moments = call(
-        image_kernel, [(mine, rows), (mine, 4 * queries)], back, message, held, scale, grads
-    )
-    late = (cols_n, mine, rows + 4 * queries)
-    late = swap(call(late_kernel, [late], spread(moments, "row", rows_n), image), "col")
-    square = pltpu.VMEM((queries, queries), jnp.float32)
+    width = pieces[2]
+    back = reduce_row(call(join_kernel, [(rows_n, mine, width + 3 * queries)], part, held))
+    image, inner = call(
+        image_kernel, [(mine, rows), (mine, queries)], back, message, held, scale, grads
+    )
+    both = pltpu.VMEM((2 * queries, queries), jnp.float32)
+    solved, terms = call(
+        functools.partial(first_kernel, width),
+        [(5, queries, queries), (rows, 4 * queries)],
+        back,
+        held,
+        scratch=[both],
+        dtypes=[jnp.float32, jnp.bfloat16],
+    )
+    late = (cols_n, mine, rows + queries)
+    inner = spread(inner, "row", rows_n)
+    late = call(late_kernel, [late], inner, image)
+    late = swap(late, "col")
     return call(
-        functools.partial(finish_kernel, rows),
+        finish_kernel,
         [(rows, queries), (rows, queries)],
         held,
-        late.reshape(queries, rows + 4 * queries),
-        scratch=[square, square],
+        solved,
+        terms,
+        late.reshape(queries, rows + queries),
+        scratch=[both],
     )
 
 

time: 150 us -> 145 us (0.967)
  blocking collectives: 124 us -> 109 us
  waiting for transfers between devices: 0 us -> 6.94 us
  starting transfers between devices: 0 us -> 3.54 us
    all_to_all x9 -> x8, blocking collectives: 124 us -> 109 us  [swap(): return lax.all_to_all(pieces, axis, 0, 0, tiled=True)]
    all_to_all x0 -> x1, waiting for transfers between devices: none -> 6.94 us  [swap(): return lax.all_to_all(pieces, axis, 0, 0, tiled=True)]
    all_to_all x0 -> x1, starting transfers between devices: none -> 3.54 us  [swap(): return lax.all_to_all(pieces, axis, 0, 0, tiled=True)]
    pallas_call x9 -> x11, Pallas kernels: 24.5 us -> 23.8 us  [call(): pl.pallas_call(kernel, out_shape=tuple((jax.ShapeDtypeStruct(*shape) for...]
  transfers between devices with their start and end apart: 0 -> 1, of which waited for: 0 -> 1; matrix products, arithmetic and copies ran while one was open for 0% -> 0% of each run, Pallas kernels for 0% -> 3%
where the time goes in v5:
time: 145 us; the launch traced here: 144 us
  blocking collectives  109 us (75%)
  Pallas kernels  23.8 us (16%)
  waiting for transfers between devices  6.94 us (5%)
  starting transfers between devices  3.54 us (2%)
    all_to_all x8, blocking collectives, swap(): return lax.all_to_all(pieces, axis, 0, 0, tiled=True)  109 us
    pallas_call x11, Pallas kernels, call(): pl.pallas_call(kernel, out_shape=tuple((jax.ShapeDtypeStruct(*shape) for...  23.8 us
    all_to_all x1, waiting for transfers between devices, swap(): return lax.all_to_all(pieces, axis, 0, 0, tiled=True)  6.94 us
    all_to_all x1, starting transfers between devices, swap(): return lax.all_to_all(pieces, axis, 0, 0, tiled=True)  3.54 us
  transfers between devices with their start and end apart: 1, of which 1 were waited for; matrix products, arithmetic and copies ran while one was open for 0% of the time, Pallas kernels for 3%

profile of v5, /device:TPU:1, one launch (start us, length us, event | category | flops | bytes accessed | tf_op | source)
XLA Modules:
  0.0 143.7 jit_solution(15964067531539065896)
XLA Ops:
  0.6 1.2 shard_map.59
  1.8 12.8 %all_to_all.45.parts_ref = bf16[16,8,512]{2,1,0:T(8,128)(2,1)S(1)} all-to-all(bf16[16,8,512]{2,1,0:T(8,128)(2,1)S(1)} %get-tuple-element.13), channel_id=1, replica_groups=mesh['row'=16,'col'=16] {'row'}, dimensions={0} | all-to-all | bytes 262144 | tf_op jit(solution)/shard_map/all_to_all | solution.py:58
  14.7 9.3 %all_to_all.46.chosen_ref = bf16[16,8,512]{2,1,0:T(8,128)(2,1)S(1)} all-to-all(bf16[16,8,512]{2,1,0:T(8,128)(2,1)S(1)} %shard_map.60), channel_id=1, replica_groups=mesh['row'=16,'col'=16] {'row'}, dimensions={0} | all-to-all | bytes 262144 | tf_op jit(solution)/shard_map/all_to_all | solution.py:58
  23.9 5.0 %shard_map.61 = (f32[8,512]{1,0:T(8,128)S(1)}, f32[16,8,512]{2,1,0:T(8,128)S(1)}, bf16[512,8192]{1,0:T(8,128)(2,1)S(1)}) custom-call(bf16[16,8,512]{2,1,0:T(8,128)(2,1)S(1)} %all_to_all.46.chosen_ref, f32[1,512]{1,0:T(1,128)S(1)} %get-tuple-element.14.scale_ref, bf16[512,8192]{1,0:T(8,128)(2,1)} %grads_hbm.1), custom_call_target="tpu_custom_call" | custom-call | tf_op jit(solution)/shard_map/pallas_call | solution.py:305
  28.9 10.4 %all_to_all.47.parts_ref = f32[16,8,512]{2,1,0:T(8,128)S(1)} all-to-all(f32[16,8,512]{2,1,0:T(8,128)S(1)} %get-tuple-element.15), channel_id=1, replica_groups=mesh['row'=16,'col'=16] {'row'}, dimensions={0} | all-to-all | bytes 524288 | tf_op jit(solution)/shard_map/all_to_all | solution.py:58
  39.3 10.6 %all_to_all.48.back_ref = f32[16,8,512]{2,1,0:T(8,128)S(1)} all-to-all(f32[16,8,512]{2,1,0:T(8,128)S(1)} %shard_map.62), channel_id=1, replica_groups=mesh['row'=16,'col'=16] {'row'}, dimensions={0} | all-to-all | bytes 524288 | tf_op jit(solution)/shard_map/all_to_all | solution.py:58
  50.0 3.4 %shard_map.63 = (f32[8,1152]{1,0:T(8,128)S(1)}, f32[16,8,512]{2,1,0:T(8,128)S(1)}) custom-call(f32[16,8,512]{2,1,0:T(8,128)S(1)} %all_to_all.48.back_ref, bf16[16,8,512]{2,1,0:T(8,128)(2,1)S(1)} %all_to_all.46.chosen_ref, f32[8,512]{1,0:T(8,128)S(1)} %get-tuple-element.16.base_ref, f32[1,512]{1,0:T(1,128)S(1)} %get-tuple-element.14.scale_ref, ...), custom_call_target="tpu_custom_call" | custom-call | tf_op jit(solution)/shard_map/pallas_call | solution.py:305
  53.5 28.5 %all_to_all.49 = f32[16,8,1152]{2,1,0:T(8,128)S(1)} all-to-all(f32[16,8,1152]{2,1,0:T(8,128)S(1)} %broadcast_in_dim.4), channel_id=1, replica_groups=mesh['row'=16,'col'=16] {'col'}, dimensions={0} | all-to-all | bytes 1179648 | tf_op jit(solution)/shard_map/all_to_all | solution.py:58
  81.9 0.8 shard_map.64
  82.7 14.8 %all_to_all.50.parts_ref = f32[16,8,896]{2,1,0:T(8,128)S(1)} all-to-all(f32[16,8,896]{2,1,0:T(8,128)S(1)} %shard_map.64), channel_id=1, replica_groups=mesh['row'=16,'col'=16] {'row'}, dimensions={0} | all-to-all | bytes 917504 | tf_op jit(solution)/shard_map/all_to_all | solution.py:58
  97.6 12.7 %all_to_all.51.back_ref = f32[16,8,896]{2,1,0:T(8,128)S(1)} all-to-all(f32[16,8,896]{2,1,0:T(8,128)S(1)} %shard_map.65), channel_id=1, replica_groups=mesh['row'=16,'col'=16] {'row'}, dimensions={0} | all-to-all | bytes 917504 | tf_op jit(solution)/shard_map/all_to_all | solution.py:58
  110.3 2.7 %shard_map.67 = (f32[8,512]{1,0:T(8,128)S(1)}, f32[8,128]{1,0:T(8,128)S(1)}) custom-call(f32[16,8,896]{2,1,0:T(8,128)S(1)} %all_to_all.51.back_ref, f32[8,1152]{1,0:T(8,128)S(1)} %get-tuple-element.18.message_ref, f32[128,1152]{1,0:T(8,128)S(1)} %bitcast.4, f32[1,512]{1,0:T(1,128)S(1)} %get-tuple-element.14.scale_ref, ...), custom_call_target="tpu_custom_call" | custom-call | tf_op jit(solution)/shard_map/pallas_call | solution.py:305
  113.1 9.6 %all_to_all.52.parts_ref = f32[16,8,128]{2,1,0:T(8,128)S(1)} all-to-all(f32[16,8,128]{2,1,0:T(8,128)S(1)} %broadcast_in_dim.5), channel_id=1, replica_groups=mesh['row'=16,'col'=16] {'row'}, dimensions={0} | all-to-all | bytes 131072 | tf_op jit(solution)/shard_map/all_to_all | solution.py:58
  122.6 0.8 shard_map.68
  123.4 3.5 %all-to-all-start.8 = ((f32[16,8,640]{2,1,0:T(8,128)}), f32[16,8,640]{2,1,0:T(8,128)S(1)}, u32[]{:S(2)}, u32[]{:S(2)}) async-start(f32[16,8,640]{2,1,0:T(8,128)} %shard_map.68), calls=%async_computation.8 | async-start | bytes 655360 | tf_op jit(solution)/shard_map/all_to_all | solution.py:58
  127.0 4.6 %shard_map.66 = (f32[5,128,128]{2,1,0:T(8,128)S(1)}, bf16[512,512]{1,0:T(8,128)(2,1)S(1)}) custom-call(f32[16,8,896]{2,1,0:T(8,128)S(1)} %all_to_all.51.back_ref, f32[128,1152]{1,0:T(8,128)S(1)} %bitcast.5), custom_call_target="tpu_custom_call" | custom-call | tf_op jit(solution)/shard_map/pallas_call | solution.py:305
  131.6 6.9 %all-to-all-done.8 = f32[16,8,640]{2,1,0:T(8,128)S(1)} async-done(((f32[16,8,640]{2,1,0:T(8,128)}), f32[16,8,640]{2,1,0:T(8,128)S(1)}, u32[]{:S(2)}, u32[]{:S(2)}) %all-to-all-start.8) | async-done | bytes 327712 | tf_op jit(solution)/shard_map/all_to_all | solution.py:58
  138.5 5.2 %shard_map.69 = (f32[512,128]{1,0:T(8,128)}, f32[512,128]{1,0:T(8,128)}) custom-call(f32[128,1152]{1,0:T(8,128)S(1)} %bitcast.6, f32[5,128,128]{2,1,0:T(8,128)S(1)} %get-tuple-element.20.solved_ref, bf16[512,512]{1,0:T(8,128)(2,1)S(1)} %get-tuple-element.21.terms_ref, f32[128,640]{1,0:T(8,128)S(1)} %bitcast.7), custom_call_target="tpu_custom_call" | custom-call | tf_op jit(solution)/shard_map/pallas_call | solution.py:305
  (5 shorter events, 0.2 us)
Async XLA Ops:
  123.4 15.1 %all-to-all-start.8 = ((f32[16,8,640]{2,1,0:T(8,128)}), f32[16,8,640]{2,1,0:T(8,128)S(1)}, u32[]{:S(2)}, u32[]{:S(2)}) async-start(f32[16,8,640]{2,1,0:T(8,128)} %shard_map.68), calls=%async_computation.8 | async-start | bytes 655360 | tf_op jit(solution)/shard_map/all_to_all | solution.py:58

commit v6 on v5

--- a/solution.py
+++ b/solution.py
@@ -7,14 +7,15 @@
 from jax.experimental.pallas import tpu as pltpu
 from jax.sharding import PartitionSpec as P
 
+
 damping = 0.5
 
 
-def full(left, right, dims=((1,), (0,))):
+def full(left, right):
     return lax.dot_general(
         left,
         right,
-        (dims, ((), ())),
+        (((1,), (0,)), ((), ())),
         precision=lax.Precision.HIGHEST,
         preferred_element_type=jnp.float32,
     )
@@ -54,6 +55,22 @@
     return both[:, :columns] + both[:, columns:]
 
 
+def row_product(left, right):
+    high, low = halves(right)
+    rows = right.shape[0]
+    both = bf16_dot(
+        jnp.concatenate(halves(left), axis=1),
+        jnp.concatenate(
+            [
+                jnp.concatenate([high, high], axis=1),
+                jnp.concatenate([low, jnp.zeros_like(low)], axis=1),
+            ]
+        ),
+        1,
+    )
+    return both[:, :rows] + both[:, rows:]
+
+
 def swap(pieces, axis):
     return lax.all_to_all(pieces, axis, 0, 0, tiled=True)
 
@@ -69,7 +86,7 @@
     down = lax.rsqrt(jnp.sum(on_diag, axis=1, keepdims=True))
     unit = mat * across * down
     reach = jnp.sum(jnp.abs(unit), axis=1, keepdims=True)
-    share = 1.0 / jnp.max(reach, axis=0, keepdims=True)
+    share = 1.8 / jnp.max(reach, axis=0, keepdims=True)
     left = eye - share * unit
     inv = share * (eye + left)
     left = product(left, left)
@@ -85,7 +102,7 @@
 
     def open_still(state):
         count, remainder = state
-        return jnp.logical_and(count < 40, remainder > 1e-5)
+        return jnp.logical_and(count < 40, remainder > 3e-4)
 
     def again(state):
         inv, left = advance(both_ref[:size], both_ref[size:])
@@ -214,10 +231,10 @@
 def join_kernel(part_ref, held_ref, out_ref):
     parts, lead, width = part_ref.shape
     rows = (held_ref.shape[1] - 128) // 2
-    base = held_ref[:, :rows]
-    other = held_ref[:, rows : 2 * rows]
-    last = ((1,), (1,))
-    inner = [full(base, base, last), full(other, base, last), full(other, other, last)]
+    queries = held_ref.shape[0]
+    stacked = jnp.concatenate([held_ref[:, :rows], held_ref[:, rows : 2 * rows]])
+    square = row_product(stacked, stacked)
+    inner = [square[:queries, :queries], square[queries:, :queries], square[queries:, queries:]]
     for k in range(parts):
         out_ref[k, :, :width] = part_ref[k]
         for n, mat in enumerate(inner):
@@ -231,7 +248,7 @@
     own_other = message_ref[:, rows : 2 * rows]
     image = scale_ref[...] * project(back_ref, grads_ref, width) + damping * own_other
     image_ref[...] = image
-    inner_ref[...] = full(image, held_ref[:, rows : 2 * rows], ((1,), (1,)))
+    inner_ref[...] = row_product(image, held_ref[:, rows : 2 * rows])
 
 
 def first_kernel(width, back_ref, held_ref, solved_ref, terms_ref, both_ref):
@@ -258,11 +275,14 @@
     for k, mat in enumerate([alpha, second, fresh, mixed, product(tab, mixed)]):
         solved_ref[k] = mat
     for k in range(2):
-        block = held_ref[:, k * rows : (k + 1) * rows].T
-        terms_ref[:, 2 * k * queries : 2 * (k + 1) * queries] = jnp.concatenate(halves(block), axis=1)
-
-
-def finish_kernel(held_ref, solved_ref, terms_ref, late_ref, solution_ref, residual_ref, both_ref):
+        high, low = halves(held_ref[:, k * rows : (k + 1) * rows].T)
+        for n, term in enumerate([high, low, high]):
+            terms_ref[:, (3 * k + n) * queries : (3 * k + n + 1) * queries] = term
+
+
+def finish_kernel(
+    held_ref, solved_ref, terms_ref, late_ref, solution_hbm, residual_hbm, both_ref, out_ref, sems
+):
     queries = held_ref.shape[0]
     rows = terms_ref.shape[0]
     tat = late_ref[:, rows:]
@@ -273,42 +293,44 @@
     eye = jnp.where(row_id == lax.broadcasted_iota(jnp.int32, shape, 1), 1.0, 0.0)
     curv = product(second.T, lead + product(tat, second))
     curv = 0.5 * (curv + curv.T)
-    image = jnp.concatenate(halves(late_ref[:, :rows].T), axis=1)
+    high, low = halves(late_ref[:, :rows].T)
+    image = jnp.concatenate([high, low, high], axis=1)
     inv = inverse_spd(curv, eye, both_ref)
     alpha_next = solve_with(curv, inv, fresh)
     gain = product(jnp.concatenate([mixed, second]), alpha_next)
     gain, gain_other = gain[:queries], gain[queries:]
     shift = per_step * gain
-
-    def times(terms, right):
-        high, low = halves(right)
-        both = jnp.dot(
-            terms,
-            jnp.concatenate(
-                [
-                    jnp.concatenate([high, low], axis=1),
-                    jnp.concatenate([high, jnp.zeros_like(low)], axis=1),
-                ]
-            ),
-            preferred_element_type=jnp.float32,
-        )
-        return both[:, : right.shape[1]] + both[:, right.shape[1] :]
-
-    first = eye - second
-    out = times(terms_ref[:, : 2 * queries], jnp.concatenate([alpha + gain, first - shift], axis=1))
-    out += times(terms_ref[:, 2 * queries :], jnp.concatenate([gain_other, second + shift], axis=1))
-    solution_ref[...] = out[:, :queries]
-    residual_ref[...] = out[:, queries:] - times(image, gain_other)
-
-
-def call(kernel, shapes, *args, scratch=(), dtypes=(jnp.float32, jnp.float32), limit=8):
+    weights = []
+    for pair in (
+        (alpha + gain, eye - second - shift),
+        (gain_other, second + shift),
+        (jnp.zeros(shape, jnp.float32), -gain_other),
+    ):
+        high, low = halves(jnp.concatenate(pair, axis=1))
+        weights += [high, high, low]
+    weights = jnp.concatenate(weights)
+    copies = []
+    step = rows // 2
+    for k in range(2):
+        block = pl.ds(k * step, step)
+        terms = jnp.concatenate([terms_ref[block], image[k * step : (k + 1) * step]], axis=1)
+        out_ref[block] = jnp.dot(terms, weights, preferred_element_type=jnp.float32)
+        for n, target in enumerate([solution_hbm, residual_hbm]):
+            source = out_ref.at[block, pl.ds(n * queries, queries)]
+            copies.append(pltpu.make_async_copy(source, target.at[block], sems.at[2 * k + n]))
+            copies[-1].start()
+    for copy in copies:
+        copy.wait()
+
+
+def call(kernel, shapes, *args, scratch=(), dtypes=(jnp.float32, jnp.float32), out_space=pltpu.VMEM):
     outs = pl.pallas_call(
         kernel,
         out_shape=tuple(jax.ShapeDtypeStruct(*shape) for shape in zip(shapes, dtypes)),
         in_specs=[pl.BlockSpec(memory_space=pltpu.VMEM if near else pl.ANY) for near, _ in map(place, args)],
-        out_specs=tuple(pl.BlockSpec(memory_space=pltpu.VMEM) for _ in shapes),
+        out_specs=tuple(pl.BlockSpec(memory_space=out_space) for _ in shapes),
         scratch_shapes=scratch,
-        compiler_params=pltpu.CompilerParams(vmem_limit_bytes=limit * 2**20),
+        compiler_params=pltpu.CompilerParams(vmem_limit_bytes=2**23),
     )(*(value for _, value in map(place, args)))
     return outs if len(outs) > 1 else outs[0]
 
@@ -372,7 +394,7 @@
     both = pltpu.VMEM((2 * queries, queries), jnp.float32)
     solved, terms = call(
         functools.partial(first_kernel, width),
-        [(5, queries, queries), (rows, 4 * queries)],
+        [(5, queries, queries), (rows, 6 * queries)],
         back,
         held,
         scratch=[both],
@@ -389,7 +411,8 @@
         solved,
         terms,
         late.reshape(queries, rows + queries),
-        scratch=[both],
+        scratch=[both, pltpu.VMEM((rows, 2 * queries), jnp.float32), pltpu.SemaphoreType.DMA((4,))],
+        out_space=pl.ANY,
     )
 
 

time: 145 us -> 144 us (level)
  no operation moved by 1% of the time
where the time goes in v6:
time: 144 us; the launch traced here: 143 us
  blocking collectives  109 us (76%)
  Pallas kernels  22.5 us (16%)
  waiting for transfers between devices  7.42 us (5%)
  starting transfers between devices  3.54 us (2%)
    all_to_all x8, blocking collectives, swap(): return lax.all_to_all(pieces, axis, 0, 0, tiled=True)  109 us
    pallas_call x11, Pallas kernels, call(): pl.pallas_call(kernel, out_shape=tuple((jax.ShapeDtypeStruct(*shape) for...  22.5 us
    all_to_all x1, waiting for transfers between devices, swap(): return lax.all_to_all(pieces, axis, 0, 0, tiled=True)  7.42 us
    all_to_all x1, starting transfers between devices, swap(): return lax.all_to_all(pieces, axis, 0, 0, tiled=True)  3.54 us
  transfers between devices with their start and end apart: 1, of which 1 were waited for; matrix products, arithmetic and copies ran while one was open for 0% of the time, Pallas kernels for 3%

profile of v6, /device:TPU:1, one launch (start us, length us, event | category | flops | bytes accessed | tf_op | source)
XLA Modules:
  0.0 142.8 jit_solution(16420218013249080485)
XLA Ops:
  0.6 1.2 shard_map.59
  1.8 12.8 %all_to_all.45.parts_ref = bf16[16,8,512]{2,1,0:T(8,128)(2,1)S(1)} all-to-all(bf16[16,8,512]{2,1,0:T(8,128)(2,1)S(1)} %get-tuple-element.13), channel_id=1, replica_groups=mesh['row'=16,'col'=16] {'row'}, dimensions={0} | all-to-all | bytes 262144 | tf_op jit(solution)/shard_map/all_to_all | solution.py:75
  14.7 9.3 %all_to_all.46.chosen_ref = bf16[16,8,512]{2,1,0:T(8,128)(2,1)S(1)} all-to-all(bf16[16,8,512]{2,1,0:T(8,128)(2,1)S(1)} %shard_map.60), channel_id=1, replica_groups=mesh['row'=16,'col'=16] {'row'}, dimensions={0} | all-to-all | bytes 262144 | tf_op jit(solution)/shard_map/all_to_all | solution.py:75
  23.9 5.0 %shard_map.61 = (f32[8,512]{1,0:T(8,128)S(1)}, f32[16,8,512]{2,1,0:T(8,128)S(1)}, bf16[512,8192]{1,0:T(8,128)(2,1)S(1)}) custom-call(bf16[16,8,512]{2,1,0:T(8,128)(2,1)S(1)} %all_to_all.46.chosen_ref, f32[1,512]{1,0:T(1,128)S(1)} %get-tuple-element.14.scale_ref, bf16[512,8192]{1,0:T(8,128)(2,1)} %grads_hbm.1), custom_call_target="tpu_custom_call" | custom-call | tf_op jit(solution)/shard_map/pallas_call | solution.py:327
  28.9 10.4 %all_to_all.47.parts_ref = f32[16,8,512]{2,1,0:T(8,128)S(1)} all-to-all(f32[16,8,512]{2,1,0:T(8,128)S(1)} %get-tuple-element.15), channel_id=1, replica_groups=mesh['row'=16,'col'=16] {'row'}, dimensions={0} | all-to-all | bytes 524288 | tf_op jit(solution)/shard_map/all_to_all | solution.py:75
  39.3 10.6 %all_to_all.48.back_ref = f32[16,8,512]{2,1,0:T(8,128)S(1)} all-to-all(f32[16,8,512]{2,1,0:T(8,128)S(1)} %shard_map.62), channel_id=1, replica_groups=mesh['row'=16,'col'=16] {'row'}, dimensions={0} | all-to-all | bytes 524288 | tf_op jit(solution)/shard_map/all_to_all | solution.py:75
  50.0 3.4 %shard_map.63 = (f32[8,1152]{1,0:T(8,128)S(1)}, f32[16,8,512]{2,1,0:T(8,128)S(1)}) custom-call(f32[16,8,512]{2,1,0:T(8,128)S(1)} %all_to_all.48.back_ref, bf16[16,8,512]{2,1,0:T(8,128)(2,1)S(1)} %all_to_all.46.chosen_ref, f32[8,512]{1,0:T(8,128)S(1)} %get-tuple-element.16.base_ref, f32[1,512]{1,0:T(1,128)S(1)} %get-tuple-element.14.scale_ref, ...), custom_call_target="tpu_custom_call" | custom-call | tf_op jit(solution)/shard_map/pallas_call | solution.py:327
  53.5 28.5 %all_to_all.49 = f32[16,8,1152]{2,1,0:T(8,128)S(1)} all-to-all(f32[16,8,1152]{2,1,0:T(8,128)S(1)} %broadcast_in_dim.4), channel_id=1, replica_groups=mesh['row'=16,'col'=16] {'col'}, dimensions={0} | all-to-all | bytes 1179648 | tf_op jit(solution)/shard_map/all_to_all | solution.py:75
  81.9 0.5 shard_map.64
  82.4 14.8 %all_to_all.50.parts_ref = f32[16,8,896]{2,1,0:T(8,128)S(1)} all-to-all(f32[16,8,896]{2,1,0:T(8,128)S(1)} %shard_map.64), channel_id=1, replica_groups=mesh['row'=16,'col'=16] {'row'}, dimensions={0} | all-to-all | bytes 917504 | tf_op jit(solution)/shard_map/all_to_all | solution.py:75
  97.3 12.7 %all_to_all.51.back_ref = f32[16,8,896]{2,1,0:T(8,128)S(1)} all-to-all(f32[16,8,896]{2,1,0:T(8,128)S(1)} %shard_map.65), channel_id=1, replica_groups=mesh['row'=16,'col'=16] {'row'}, dimensions={0} | all-to-all | bytes 917504 | tf_op jit(solution)/shard_map/all_to_all | solution.py:75
  110.0 2.5 %shard_map.67 = (f32[8,512]{1,0:T(8,128)S(1)}, f32[8,128]{1,0:T(8,128)S(1)}) custom-call(f32[16,8,896]{2,1,0:T(8,128)S(1)} %all_to_all.51.back_ref, f32[8,1152]{1,0:T(8,128)S(1)} %get-tuple-element.18.message_ref, f32[128,1152]{1,0:T(8,128)S(1)} %bitcast.4, f32[1,512]{1,0:T(1,128)S(1)} %get-tuple-element.14.scale_ref, ...), custom_call_target="tpu_custom_call" | custom-call | tf_op jit(solution)/shard_map/pallas_call | solution.py:327
  112.5 9.6 %all_to_all.52.parts_ref = f32[16,8,128]{2,1,0:T(8,128)S(1)} all-to-all(f32[16,8,128]{2,1,0:T(8,128)S(1)} %broadcast_in_dim.5), channel_id=1, replica_groups=mesh['row'=16,'col'=16] {'row'}, dimensions={0} | all-to-all | bytes 131072 | tf_op jit(solution)/shard_map/all_to_all | solution.py:75
  122.1 0.8 shard_map.68
  122.8 3.5 %all-to-all-start.8 = ((f32[16,8,640]{2,1,0:T(8,128)}), f32[16,8,640]{2,1,0:T(8,128)S(1)}, u32[]{:S(2)}, u32[]{:S(2)}) async-start(f32[16,8,640]{2,1,0:T(8,128)} %shard_map.68), calls=%async_computation.8 | async-start | bytes 655360 | tf_op jit(solution)/shard_map/all_to_all | solution.py:75
  126.4 4.1 %shard_map.66 = (f32[5,128,128]{2,1,0:T(8,128)S(1)}, bf16[512,768]{1,0:T(8,128)(2,1)S(1)}) custom-call(f32[16,8,896]{2,1,0:T(8,128)S(1)} %all_to_all.51.back_ref, f32[128,1152]{1,0:T(8,128)S(1)} %bitcast.5), custom_call_target="tpu_custom_call" | custom-call | tf_op jit(solution)/shard_map/pallas_call | solution.py:327
  130.5 7.4 %all-to-all-done.8 = f32[16,8,640]{2,1,0:T(8,128)S(1)} async-done(((f32[16,8,640]{2,1,0:T(8,128)}), f32[16,8,640]{2,1,0:T(8,128)S(1)}, u32[]{:S(2)}, u32[]{:S(2)}) %all-to-all-start.8) | async-done | bytes 327712 | tf_op jit(solution)/shard_map/all_to_all | solution.py:75
  137.9 4.9 %shard_map.69 = (f32[512,128]{1,0:T(8,128)}, f32[512,128]{1,0:T(8,128)}) custom-call(f32[128,1152]{1,0:T(8,128)S(1)} %bitcast.6, f32[5,128,128]{2,1,0:T(8,128)S(1)} %get-tuple-element.20.solved_ref, bf16[512,768]{1,0:T(8,128)(2,1)S(1)} %get-tuple-element.21.terms_ref, f32[128,640]{1,0:T(8,128)S(1)} %bitcast.7), custom_call_target="tpu_custom_call" | custom-call | tf_op jit(solution)/shard_map/pallas_call | solution.py:327
  (5 shorter events, 0.2 us)
Async XLA Ops:
  122.8 15.1 %all-to-all-start.8 = ((f32[16,8,640]{2,1,0:T(8,128)}), f32[16,8,640]{2,1,0:T(8,128)S(1)}, u32[]{:S(2)}, u32[]{:S(2)}) async-start(f32[16,8,640]{2,1,0:T(8,128)} %shard_map.68), calls=%async_computation.8 | async-start | bytes 655360 | tf_op jit(solution)/shard_map/all_to_all | solution.py:75

commit v7 on v6

--- a/solution.py
+++ b/solution.py
@@ -181,7 +181,9 @@
         part_ref[k] = both_terms(product)
 
 
-def base_kernel(chosen_ref, scale_ref, grads_hbm, base_ref, part_ref, grads_ref, sems):
+def base_kernel(
+    chosen_ref, scale_ref, grads_hbm, base_ref, part_ref, grads_ref, turned_ref, sems
+):
     parts, _, width = chosen_ref.shape
     copies = []
     for k in range(parts):
@@ -191,23 +193,27 @@
     total = jnp.zeros(base_ref.shape, jnp.float32)
     for k in range(parts):
         copies[k].wait()
-        total += bf16_dot(chosen_ref[k], grads_ref[:, k * width : (k + 1) * width], 1)
+        turned = grads_ref[:, k * width : (k + 1) * width].T
+        turned_ref[k * width : (k + 1) * width] = turned
+        total += bf16_dot(chosen_ref[k], turned, 0)
     scale = scale_ref[...]
     base = scale * total
     base_ref[...] = base
     partial_back(scale * base, grads_ref, part_ref)
 
 
-def project(back_ref, grads_ref, width):
+def project(back_ref, turned_ref, width):
     parts, lead, _ = back_ref.shape
-    total = jnp.zeros((2 * lead, grads_ref.shape[0]), jnp.float32)
+    total = jnp.zeros((2 * lead, turned_ref.shape[1]), jnp.float32)
     for k in range(parts):
         terms = two_terms(back_ref[k, :, :width])
-        total += bf16_dot(terms, grads_ref[:, k * width : (k + 1) * width], 1)
+        total += bf16_dot(terms, turned_ref[k * width : (k + 1) * width], 0)
     return both_terms(total)
 
 
-def other_kernel(back_ref, chosen_ref, base_ref, scale_ref, grads_ref, message_ref, part_ref):
+def other_kernel(
+    back_ref, chosen_ref, base_ref, scale_ref, grads_ref, turned_ref, message_ref, part_ref
+):
     parts, lead, width = back_ref.shape
     rows = base_ref.shape[1]
     square = jnp.zeros((lead, width), jnp.float32)
@@ -221,7 +227,7 @@
     step = square / (curve + damping * square)
     base = base_ref[...]
     scale = scale_ref[...]
-    other = base - step * (scale * project(back_ref, grads_ref, width) + damping * base)
+    other = base - step * (scale * project(back_ref, turned_ref, width) + damping * base)
     message_ref[:, :rows] = base
     message_ref[:, rows : 2 * rows] = other
     message_ref[:, 2 * rows :] = jnp.broadcast_to(step, (lead, message_ref.shape[1] - 2 * rows))
@@ -242,11 +248,11 @@
             out_ref[k, :, lanes] = mat[k * lead : (k + 1) * lead]
 
 
-def image_kernel(back_ref, message_ref, held_ref, scale_ref, grads_ref, image_ref, inner_ref):
+def image_kernel(back_ref, message_ref, held_ref, scale_ref, turned_ref, image_ref, inner_ref):
     rows = image_ref.shape[1]
-    width = grads_ref.shape[1] // back_ref.shape[0]
+    width = turned_ref.shape[0] // back_ref.shape[0]
     own_other = message_ref[:, rows : 2 * rows]
-    image = scale_ref[...] * project(back_ref, grads_ref, width) + damping * own_other
+    image = scale_ref[...] * project(back_ref, turned_ref, width) + damping * own_other
     image_ref[...] = image
     inner_ref[...] = row_product(image, held_ref[:, rows : 2 * rows])
 
@@ -373,23 +379,23 @@
         dtypes=[bank.dtype, jnp.float32],
     )
     chosen = reduce_row(picked)
-    base, part, grads = call(
+    base, part, grads, turned = call(
         base_kernel,
-        [(mine, rows), pieces, grads.shape],
+        [(mine, rows), pieces, grads.shape, (depth, rows)],
         chosen,
         scale,
         Far(grads),
         scratch=[pltpu.SemaphoreType.DMA((rows_n,))],
-        dtypes=[jnp.float32, jnp.float32, grads.dtype],
+        dtypes=[jnp.float32, jnp.float32, grads.dtype, grads.dtype],
     )
     back = reduce_row(part)
     wide = 2 * rows + lanes
-    message, part = call(other_kernel, [(mine, wide), pieces], back, chosen, base, scale, grads)
+    message, part = call(other_kernel, [(mine, wide), pieces], back, chosen, base, scale, grads, turned)
     held = spread(message, "col", cols_n).reshape(queries, wide)
     width = pieces[2]
     back = reduce_row(call(join_kernel, [(rows_n, mine, width + 3 * queries)], part, held))
     image, inner = call(
-        image_kernel, [(mine, rows), (mine, queries)], back, message, held, scale, grads
+        image_kernel, [(mine, rows), (mine, queries)], back, message, held, scale, turned
     )
     both = pltpu.VMEM((2 * queries, queries), jnp.float32)
     solved, terms = call(

time: 144 us -> 142 us (0.986)
  no operation moved by 1% of the time
where the time goes in v7:
time: 142 us; the launch traced here: 141 us
  blocking collectives  109 us (77%)
  Pallas kernels  21.1 us (15%)
  waiting for transfers between devices  7.25 us (5%)
  starting transfers between devices  3.54 us (2%)
    all_to_all x8, blocking collectives, swap(): return lax.all_to_all(pieces, axis, 0, 0, tiled=True)  109 us
    pallas_call x11, Pallas kernels, call(): pl.pallas_call(kernel, out_shape=tuple((jax.ShapeDtypeStruct(*shape) for...  21.1 us
    all_to_all x1, waiting for transfers between devices, swap(): return lax.all_to_all(pieces, axis, 0, 0, tiled=True)  7.25 us
    all_to_all x1, starting transfers between devices, swap(): return lax.all_to_all(pieces, axis, 0, 0, tiled=True)  3.54 us
  transfers between devices with their start and end apart: 1, of which 1 were waited for; matrix products, arithmetic and copies ran while one was open for 0% of the time, Pallas kernels for 3%

profile of v7, /device:TPU:1, one launch (start us, length us, event | category | flops | bytes accessed | tf_op | source)
XLA Modules:
  0.0 141.4 jit_solution(15142259175807826198)
XLA Ops:
  0.6 1.2 shard_map.59
  1.8 12.8 %all_to_all.45.parts_ref = bf16[16,8,512]{2,1,0:T(8,128)(2,1)S(1)} all-to-all(bf16[16,8,512]{2,1,0:T(8,128)(2,1)S(1)} %get-tuple-element.14), channel_id=1, replica_groups=mesh['row'=16,'col'=16] {'row'}, dimensions={0} | all-to-all | bytes 262144 | tf_op jit(solution)/shard_map/all_to_all | solution.py:75
  14.7 9.3 %all_to_all.46.chosen_ref = bf16[16,8,512]{2,1,0:T(8,128)(2,1)S(1)} all-to-all(bf16[16,8,512]{2,1,0:T(8,128)(2,1)S(1)} %shard_map.60), channel_id=1, replica_groups=mesh['row'=16,'col'=16] {'row'}, dimensions={0} | all-to-all | bytes 262144 | tf_op jit(solution)/shard_map/all_to_all | solution.py:75
  23.9 5.6 %shard_map.61 = (f32[8,512]{1,0:T(8,128)S(1)}, f32[16,8,512]{2,1,0:T(8,128)S(1)}, bf16[512,8192]{1,0:T(8,128)(2,1)S(1)}, bf16[8192,512]{1,0:T(8,128)(2,1)S(1)}) custom-call(bf16[16,8,512]{2,1,0:T(8,128)(2,1)S(1)} %all_to_all.46.chosen_ref, f32[1,512]{1,0:T(1,128)S(1)} %get-tuple-element.15.scale_ref, bf16[512,8192]{1,0:T(8,128)(2,1)} %grads_hbm.1), custom_call_target="tpu_custom_call" | custom-call | tf_op jit(solution)/shard_map/pallas_call | solution.py:333
  29.5 10.4 %all_to_all.47.parts_ref = f32[16,8,512]{2,1,0:T(8,128)S(1)} all-to-all(f32[16,8,512]{2,1,0:T(8,128)S(1)} %get-tuple-element.16), channel_id=1, replica_groups=mesh['row'=16,'col'=16] {'row'}, dimensions={0} | all-to-all | bytes 524288 | tf_op jit(solution)/shard_map/all_to_all | solution.py:75
  39.9 10.6 %all_to_all.48.back_ref = f32[16,8,512]{2,1,0:T(8,128)S(1)} all-to-all(f32[16,8,512]{2,1,0:T(8,128)S(1)} %shard_map.62), channel_id=1, replica_groups=mesh['row'=16,'col'=16] {'row'}, dimensions={0} | all-to-all | bytes 524288 | tf_op jit(solution)/shard_map/all_to_all | solution.py:75
  50.6 2.4 %shard_map.63 = (f32[8,1152]{1,0:T(8,128)S(1)}, f32[16,8,512]{2,1,0:T(8,128)S(1)}) custom-call(f32[16,8,512]{2,1,0:T(8,128)S(1)} %all_to_all.48.back_ref, bf16[16,8,512]{2,1,0:T(8,128)(2,1)S(1)} %all_to_all.46.chosen_ref, f32[8,512]{1,0:T(8,128)S(1)} %get-tuple-element.17.base_ref, f32[1,512]{1,0:T(1,128)S(1)} %get-tuple-element.15.scale_ref, ...), custom_call_target="tpu_custom_call" | custom-call | tf_op jit(solution)/shard_map/pallas_call | solution.py:333
  53.0 28.5 %all_to_all.49 = f32[16,8,1152]{2,1,0:T(8,128)S(1)} all-to-all(f32[16,8,1152]{2,1,0:T(8,128)S(1)} %broadcast_in_dim.4), channel_id=1, replica_groups=mesh['row'=16,'col'=16] {'col'}, dimensions={0} | all-to-all | bytes 1179648 | tf_op jit(solution)/shard_map/all_to_all | solution.py:75
  81.4 0.5 shard_map.64
  81.9 14.8 %all_to_all.50.parts_ref = f32[16,8,896]{2,1,0:T(8,128)S(1)} all-to-all(f32[16,8,896]{2,1,0:T(8,128)S(1)} %shard_map.64), channel_id=1, replica_groups=mesh['row'=16,'col'=16] {'row'}, dimensions={0} | all-to-all | bytes 917504 | tf_op jit(solution)/shard_map/all_to_all | solution.py:75
  96.8 12.7 %all_to_all.51.back_ref = f32[16,8,896]{2,1,0:T(8,128)S(1)} all-to-all(f32[16,8,896]{2,1,0:T(8,128)S(1)} %shard_map.65), channel_id=1, replica_groups=mesh['row'=16,'col'=16] {'row'}, dimensions={0} | all-to-all | bytes 917504 | tf_op jit(solution)/shard_map/all_to_all | solution.py:75
  109.5 1.4 shard_map.67
  110.9 9.6 %all_to_all.52.parts_ref = f32[16,8,128]{2,1,0:T(8,128)S(1)} all-to-all(f32[16,8,128]{2,1,0:T(8,128)S(1)} %broadcast_in_dim.5), channel_id=1, replica_groups=mesh['row'=16,'col'=16] {'row'}, dimensions={0} | all-to-all | bytes 131072 | tf_op jit(solution)/shard_map/all_to_all | solution.py:75
  120.5 0.8 shard_map.68
  121.3 3.5 %all-to-all-start.8 = ((f32[16,8,640]{2,1,0:T(8,128)}), f32[16,8,640]{2,1,0:T(8,128)S(1)}, u32[]{:S(2)}, u32[]{:S(2)}) async-start(f32[16,8,640]{2,1,0:T(8,128)} %shard_map.68), calls=%async_computation.8 | async-start | bytes 655360 | tf_op jit(solution)/shard_map/all_to_all | solution.py:75
  124.8 4.3 %shard_map.66 = (f32[5,128,128]{2,1,0:T(8,128)S(1)}, bf16[512,768]{1,0:T(8,128)(2,1)S(1)}) custom-call(f32[16,8,896]{2,1,0:T(8,128)S(1)} %all_to_all.51.back_ref, f32[128,1152]{1,0:T(8,128)S(1)} %bitcast.5), custom_call_target="tpu_custom_call" | custom-call | tf_op jit(solution)/shard_map/pallas_call | solution.py:333
  129.1 7.2 %all-to-all-done.8 = f32[16,8,640]{2,1,0:T(8,128)S(1)} async-done(((f32[16,8,640]{2,1,0:T(8,128)}), f32[16,8,640]{2,1,0:T(8,128)S(1)}, u32[]{:S(2)}, u32[]{:S(2)}) %all-to-all-start.8) | async-done | bytes 327712 | tf_op jit(solution)/shard_map/all_to_all | solution.py:75
  136.4 4.9 %shard_map.69 = (f32[512,128]{1,0:T(8,128)}, f32[512,128]{1,0:T(8,128)}) custom-call(f32[128,1152]{1,0:T(8,128)S(1)} %bitcast.6, f32[5,128,128]{2,1,0:T(8,128)S(1)} %get-tuple-element.22.solved_ref, bf16[512,768]{1,0:T(8,128)(2,1)S(1)} %get-tuple-element.23.terms_ref, f32[128,640]{1,0:T(8,128)S(1)} %bitcast.7), custom_call_target="tpu_custom_call" | custom-call | tf_op jit(solution)/shard_map/pallas_call | solution.py:333
  (5 shorter events, 0.2 us)
Async XLA Ops:
  121.3 15.1 %all-to-all-start.8 = ((f32[16,8,640]{2,1,0:T(8,128)}), f32[16,8,640]{2,1,0:T(8,128)S(1)}, u32[]{:S(2)}, u32[]{:S(2)}) async-start(f32[16,8,640]{2,1,0:T(8,128)} %shard_map.68), calls=%async_computation.8 | async-start | bytes 655360 | tf_op jit(solution)/shard_map/all_to_all | solution.py:75

commit v8 on v7

--- a/solution.py
+++ b/solution.py
@@ -234,13 +234,27 @@
     partial_back(scale * other, grads_ref, part_ref)
 
 
+def masks(size):
+    row = lax.broadcasted_iota(jnp.int32, (size, size), 0)
+    column = lax.broadcasted_iota(jnp.int32, (size, size), 1)
+    after = jnp.logical_or(column == row + 1, row == column + size - 1)
+    return column <= row, after, column == row + size - 1, column == row
+
+
 def join_kernel(part_ref, held_ref, out_ref):
     parts, lead, width = part_ref.shape
     rows = (held_ref.shape[1] - 128) // 2
     queries = held_ref.shape[0]
     stacked = jnp.concatenate([held_ref[:, :rows], held_ref[:, rows : 2 * rows]])
     square = row_product(stacked, stacked)
-    inner = [square[:queries, :queries], square[queries:, :queries], square[queries:, queries:]]
+    bb, tb, tt = square[:queries, :queries], square[queries:, :queries], square[queries:, queries:]
+    lower, after, corner, eye = masks(queries)
+    bab = 1.0 / held_ref[:, 2 * rows :] * (bb - tb)
+    on_diag = jnp.sum(jnp.where(eye, tt, 0.0), axis=1, keepdims=True)
+    inner = [
+        jnp.where(lower, bb, tt),
+        jnp.where(after, on_diag, jnp.where(jnp.logical_or(lower, corner), bab, 0.0)),
+    ]
     for k in range(parts):
         out_ref[k, :, :width] = part_ref[k]
         for n, mat in enumerate(inner):
@@ -261,16 +275,22 @@
     queries = held_ref.shape[0]
     rows = terms_ref.shape[0]
     parts = range(back_ref.shape[0])
-    bb, tb, tt = (
+    one, two = (
         jnp.concatenate([back_ref[k, :, width + n * queries : width + (n + 1) * queries] for k in parts])
-        for n in range(3)
-    )
-    per_step = 1.0 / held_ref[:, 2 * rows :]
-    shape = (queries, queries)
-    row_id = lax.broadcasted_iota(jnp.int32, shape, 0)
-    eye = jnp.where(row_id == lax.broadcasted_iota(jnp.int32, shape, 1), 1.0, 0.0)
-
-    bab = per_step * (bb - tb)
+        for n in range(2)
+    )
+    step = held_ref[:, 2 * rows :]
+    per_step = 1.0 / step
+    lower, after, corner, same = masks(queries)
+    eye = jnp.where(same, 1.0, 0.0)
+    one_t, two_t = one.T, two.T
+    bb = jnp.where(lower, one, one_t)
+    tt = jnp.where(lower, one_t, one)
+    tt = jnp.where(same, jnp.sum(jnp.where(after, two, 0.0), axis=1, keepdims=True), tt)
+    plain = jnp.logical_or(jnp.logical_and(lower, jnp.logical_not(after)), corner)
+    bab = jnp.where(plain, two, two_t)
+
+    tb = bb - step * bab
     bat = per_step * (tb.T - tt)
     tab = bat.T
     inv = inverse_spd(bab, eye, both_ref)
@@ -393,7 +413,7 @@
     message, part = call(other_kernel, [(mine, wide), pieces], back, chosen, base, scale, grads, turned)
     held = spread(message, "col", cols_n).reshape(queries, wide)
     width = pieces[2]
-    back = reduce_row(call(join_kernel, [(rows_n, mine, width + 3 * queries)], part, held))
+    back = reduce_row(call(join_kernel, [(rows_n, mine, width + 2 * queries)], part, held))
     image, inner = call(
         image_kernel, [(mine, rows), (mine, queries)], back, message, held, scale, turned
     )

time: 142 us -> 141 us (level)
  blocking collectives: 109 us -> 107 us
where the time goes in v8:
time: 141 us; the launch traced here: 140 us
  blocking collectives  107 us (76%)
  Pallas kernels  21.2 us (15%)
  waiting for transfers between devices  7.17 us (5%)
  starting transfers between devices  3.54 us (3%)
    all_to_all x8, blocking collectives, swap(): return lax.all_to_all(pieces, axis, 0, 0, tiled=True)  107 us
    pallas_call x11, Pallas kernels, call(): pl.pallas_call(kernel, out_shape=tuple((jax.ShapeDtypeStruct(*shape) for...  21.2 us
    all_to_all x1, waiting for transfers between devices, swap(): return lax.all_to_all(pieces, axis, 0, 0, tiled=True)  7.17 us
    all_to_all x1, starting transfers between devices, swap(): return lax.all_to_all(pieces, axis, 0, 0, tiled=True)  3.54 us
  transfers between devices with their start and end apart: 1, of which 1 were waited for; matrix products, arithmetic and copies ran while one was open for 0% of the time, Pallas kernels for 3%

profile of v8, /device:TPU:1, one launch (start us, length us, event | category | flops | bytes accessed | tf_op | source)
XLA Modules:
  0.0 140.1 jit_solution(15829124596451716689)
XLA Ops:
  0.6 1.2 shard_map.59
  1.8 12.8 %all_to_all.45.parts_ref = bf16[16,8,512]{2,1,0:T(8,128)(2,1)S(1)} all-to-all(bf16[16,8,512]{2,1,0:T(8,128)(2,1)S(1)} %get-tuple-element.14), channel_id=1, replica_groups=mesh['row'=16,'col'=16] {'row'}, dimensions={0} | all-to-all | bytes 262144 | tf_op jit(solution)/shard_map/all_to_all | solution.py:75
  14.7 9.3 %all_to_all.46.chosen_ref = bf16[16,8,512]{2,1,0:T(8,128)(2,1)S(1)} all-to-all(bf16[16,8,512]{2,1,0:T(8,128)(2,1)S(1)} %shard_map.60), channel_id=1, replica_groups=mesh['row'=16,'col'=16] {'row'}, dimensions={0} | all-to-all | bytes 262144 | tf_op jit(solution)/shard_map/all_to_all | solution.py:75
  23.9 5.6 %shard_map.61 = (f32[8,512]{1,0:T(8,128)S(1)}, f32[16,8,512]{2,1,0:T(8,128)S(1)}, bf16[512,8192]{1,0:T(8,128)(2,1)S(1)}, bf16[8192,512]{1,0:T(8,128)(2,1)S(1)}) custom-call(bf16[16,8,512]{2,1,0:T(8,128)(2,1)S(1)} %all_to_all.46.chosen_ref, f32[1,512]{1,0:T(1,128)S(1)} %get-tuple-element.15.scale_ref, bf16[512,8192]{1,0:T(8,128)(2,1)} %grads_hbm.1), custom_call_target="tpu_custom_call" | custom-call | tf_op jit(solution)/shard_map/pallas_call | solution.py:353
  29.5 10.4 %all_to_all.47.parts_ref = f32[16,8,512]{2,1,0:T(8,128)S(1)} all-to-all(f32[16,8,512]{2,1,0:T(8,128)S(1)} %get-tuple-element.16), channel_id=1, replica_groups=mesh['row'=16,'col'=16] {'row'}, dimensions={0} | all-to-all | bytes 524288 | tf_op jit(solution)/shard_map/all_to_all | solution.py:75
  39.9 10.6 %all_to_all.48.back_ref = f32[16,8,512]{2,1,0:T(8,128)S(1)} all-to-all(f32[16,8,512]{2,1,0:T(8,128)S(1)} %shard_map.62), channel_id=1, replica_groups=mesh['row'=16,'col'=16] {'row'}, dimensions={0} | all-to-all | bytes 524288 | tf_op jit(solution)/shard_map/all_to_all | solution.py:75
  50.6 2.4 %shard_map.63 = (f32[8,1152]{1,0:T(8,128)S(1)}, f32[16,8,512]{2,1,0:T(8,128)S(1)}) custom-call(f32[16,8,512]{2,1,0:T(8,128)S(1)} %all_to_all.48.back_ref, bf16[16,8,512]{2,1,0:T(8,128)(2,1)S(1)} %all_to_all.46.chosen_ref, f32[8,512]{1,0:T(8,128)S(1)} %get-tuple-element.17.base_ref, f32[1,512]{1,0:T(1,128)S(1)} %get-tuple-element.15.scale_ref, ...), custom_call_target="tpu_custom_call" | custom-call | tf_op jit(solution)/shard_map/pallas_call | solution.py:353
  53.0 28.5 %all_to_all.49 = f32[16,8,1152]{2,1,0:T(8,128)S(1)} all-to-all(f32[16,8,1152]{2,1,0:T(8,128)S(1)} %broadcast_in_dim.4), channel_id=1, replica_groups=mesh['row'=16,'col'=16] {'col'}, dimensions={0} | all-to-all | bytes 1179648 | tf_op jit(solution)/shard_map/all_to_all | solution.py:75
  81.4 0.5 shard_map.64
  82.0 14.1 %all_to_all.50.parts_ref = f32[16,8,768]{2,1,0:T(8,128)S(1)} all-to-all(f32[16,8,768]{2,1,0:T(8,128)S(1)} %shard_map.64), channel_id=1, replica_groups=mesh['row'=16,'col'=16] {'row'}, dimensions={0} | all-to-all | bytes 786432 | tf_op jit(solution)/shard_map/all_to_all | solution.py:75
  96.2 12.0 %all_to_all.51.back_ref = f32[16,8,768]{2,1,0:T(8,128)S(1)} all-to-all(f32[16,8,768]{2,1,0:T(8,128)S(1)} %shard_map.65), channel_id=1, replica_groups=mesh['row'=16,'col'=16] {'row'}, dimensions={0} | all-to-all | bytes 786432 | tf_op jit(solution)/shard_map/all_to_all | solution.py:75
  108.2 1.4 shard_map.67
  109.6 9.6 %all_to_all.52.parts_ref = f32[16,8,128]{2,1,0:T(8,128)S(1)} all-to-all(f32[16,8,128]{2,1,0:T(8,128)S(1)} %broadcast_in_dim.5), channel_id=1, replica_groups=mesh['row'=16,'col'=16] {'row'}, dimensions={0} | all-to-all | bytes 131072 | tf_op jit(solution)/shard_map/all_to_all | solution.py:75
  119.1 0.8 shard_map.68
  119.9 3.5 %all-to-all-start.8 = ((f32[16,8,640]{2,1,0:T(8,128)}), f32[16,8,640]{2,1,0:T(8,128)S(1)}, u32[]{:S(2)}, u32[]{:S(2)}) async-start(f32[16,8,640]{2,1,0:T(8,128)} %shard_map.68), calls=%async_computation.8 | async-start | bytes 655360 | tf_op jit(solution)/shard_map/all_to_all | solution.py:75
  123.5 4.4 %shard_map.66 = (f32[5,128,128]{2,1,0:T(8,128)S(1)}, bf16[512,768]{1,0:T(8,128)(2,1)S(1)}) custom-call(f32[16,8,768]{2,1,0:T(8,128)S(1)} %all_to_all.51.back_ref, f32[128,1152]{1,0:T(8,128)S(1)} %bitcast.5), custom_call_target="tpu_custom_call" | custom-call | tf_op jit(solution)/shard_map/pallas_call | solution.py:353
  127.9 7.2 %all-to-all-done.8 = f32[16,8,640]{2,1,0:T(8,128)S(1)} async-done(((f32[16,8,640]{2,1,0:T(8,128)}), f32[16,8,640]{2,1,0:T(8,128)S(1)}, u32[]{:S(2)}, u32[]{:S(2)}) %all-to-all-start.8) | async-done | bytes 327712 | tf_op jit(solution)/shard_map/all_to_all | solution.py:75
  135.0 4.9 %shard_map.69 = (f32[512,128]{1,0:T(8,128)}, f32[512,128]{1,0:T(8,128)}) custom-call(f32[128,1152]{1,0:T(8,128)S(1)} %bitcast.6, f32[5,128,128]{2,1,0:T(8,128)S(1)} %get-tuple-element.22.solved_ref, bf16[512,768]{1,0:T(8,128)(2,1)S(1)} %get-tuple-element.23.terms_ref, f32[128,640]{1,0:T(8,128)S(1)} %bitcast.7), custom_call_target="tpu_custom_call" | custom-call | tf_op jit(solution)/shard_map/pallas_call | solution.py:353
  (5 shorter events, 0.2 us)
Async XLA Ops:
  119.9 15.1 %all-to-all-start.8 = ((f32[16,8,640]{2,1,0:T(8,128)}), f32[16,8,640]{2,1,0:T(8,128)S(1)}, u32[]{:S(2)}, u32[]{:S(2)}) async-start(f32[16,8,640]{2,1,0:T(8,128)} %shard_map.68), calls=%async_computation.8 | async-start | bytes 655360 | tf_op jit(solution)/shard_map/all_to_all | solution.py:75

commit v9 on v8

--- a/solution.py
+++ b/solution.py
@@ -85,17 +85,18 @@
     across = lax.rsqrt(jnp.sum(on_diag, axis=0, keepdims=True))
     down = lax.rsqrt(jnp.sum(on_diag, axis=1, keepdims=True))
     unit = mat * across * down
-    reach = jnp.sum(jnp.abs(unit), axis=1, keepdims=True)
-    share = 1.8 / jnp.max(reach, axis=0, keepdims=True)
-    left = eye - share * unit
-    inv = share * (eye + left)
-    left = product(left, left)
+    twice = product(unit, unit)
+    reach = jnp.sum(jnp.abs(twice), axis=1, keepdims=True)
+    share = 1.8 * lax.rsqrt(jnp.max(reach, axis=0, keepdims=True))
+    part = share * unit
+    inv = share * (2.0 * eye - part)
+    left = eye - 2.0 * part + share * share * twice
 
     def advance(inv, left):
         both = product(jnp.concatenate([inv, left]), left)
         return inv + both[:size], both[size:]
 
-    for _ in range(4):
+    for _ in range(3):
         inv, left = advance(inv, left)
     both_ref[:size] = inv
     both_ref[size:] = left
@@ -122,12 +123,28 @@
 
 
 def pick_kernel(
-    ids_hbm, seeds_hbm, bank_hbm, picked_ref, scale_ref, ids_ref, seeds_ref, bank_ref, sems
+    ids_hbm,
+    seeds_hbm,
+    bank_hbm,
+    grads_hbm,
+    picked_ref,
+    scale_ref,
+    begin_ref,
+    ids_ref,
+    seeds_ref,
+    bank_ref,
+    sems,
 ):
+    begin_hbm = grads_hbm.at[:, pl.ds(0, begin_ref.shape[1])]
     copies = [
         pltpu.make_async_copy(source, target, sems.at[k])
         for k, (source, target) in enumerate(
-            [(ids_hbm, ids_ref), (bank_hbm, bank_ref), (seeds_hbm, seeds_ref)]
+            [
+                (ids_hbm, ids_ref),
+                (bank_hbm, bank_ref),
+                (seeds_hbm, seeds_ref),
+                (begin_hbm, begin_ref),
+            ]
         )
     ]
     for copy in copies:
@@ -154,6 +171,7 @@
     for k in range(groups):
         seeds = seeds_ref[pl.ds(my_row * groups + k, 1), :]
         scale_ref[:, k * lanes : (k + 1) * lanes] = jnp.exp2(seeds.astype(jnp.float32) / 4.0)
+    copies[3].wait()
 
 
 def sum_kernel(parts_ref, out_ref):
@@ -182,20 +200,25 @@
 
 
 def base_kernel(
-    chosen_ref, scale_ref, grads_hbm, base_ref, part_ref, grads_ref, turned_ref, sems
+    chosen_ref, scale_ref, begin_ref, grads_hbm, base_ref, part_ref, grads_ref, turned_ref, sems
 ):
     parts, _, width = chosen_ref.shape
     copies = []
     for k in range(parts):
         block = (slice(None), pl.ds(k * width, width))
         copies.append(pltpu.make_async_copy(grads_hbm.at[block], grads_ref.at[block], sems.at[k]))
-        copies[k].start()
+    for copy in copies[1:] + copies[:1]:
+        copy.start()
     total = jnp.zeros(base_ref.shape, jnp.float32)
     for k in range(parts):
-        copies[k].wait()
-        turned = grads_ref[:, k * width : (k + 1) * width].T
+        if k == 0:
+            turned = begin_ref[...].T
+        else:
+            copies[k].wait()
+            turned = grads_ref[:, k * width : (k + 1) * width].T
         turned_ref[k * width : (k + 1) * width] = turned
         total += bf16_dot(chosen_ref[k], turned, 0)
+    copies[0].wait()
     scale = scale_ref[...]
     base = scale * total
     base_ref[...] = base
@@ -296,9 +319,10 @@
     inv = inverse_spd(bab, eye, both_ref)
     alpha = solve_with(bab, inv, bb)
     second = per_step * alpha
-    fresh = product(second.T, tb - full(tab, alpha))
+    second_t = second.T
+    fresh = product(second_t, tb - full(tab, alpha))
     mixed = -solve_with(bab, inv, product(bat, second))
-    for k, mat in enumerate([alpha, second, fresh, mixed, product(tab, mixed)]):
+    for k, mat in enumerate([alpha, second, second_t, fresh, mixed, product(tab, mixed)]):
         solved_ref[k] = mat
     for k in range(2):
         high, low = halves(held_ref[:, k * rows : (k + 1) * rows].T)
@@ -313,12 +337,11 @@
     rows = terms_ref.shape[0]
     tat = late_ref[:, rows:]
     per_step = 1.0 / held_ref[:, 2 * rows :]
-    alpha, second, fresh, mixed, lead = (solved_ref[k] for k in range(5))
+    alpha, second, second_t, fresh, mixed, lead = (solved_ref[k] for k in range(6))
     shape = (queries, queries)
     row_id = lax.broadcasted_iota(jnp.int32, shape, 0)
     eye = jnp.where(row_id == lax.broadcasted_iota(jnp.int32, shape, 1), 1.0, 0.0)
-    curv = product(second.T, lead + product(tat, second))
-    curv = 0.5 * (curv + curv.T)
+    curv = product(second_t, lead + product(tat, second))
     high, low = halves(late_ref[:, :rows].T)
     image = jnp.concatenate([high, low, high], axis=1)
     inv = inverse_spd(curv, eye, both_ref)
@@ -384,19 +407,20 @@
         return swap(total, "row")
 
     seeds = seeds.reshape(-1, lanes)
-    picked, scale = call(
+    picked, scale, begin = call(
         pick_kernel,
-        [pieces, (1, rows)],
+        [pieces, (1, rows), (rows, pieces[2])],
         Far(query_ids),
         Far(seeds),
         Far(bank),
+        Far(grads),
         scratch=[
             pltpu.SMEM(query_ids.shape, jnp.int32),
             pltpu.VMEM(seeds.shape, jnp.int32),
             pltpu.VMEM(bank.shape, bank.dtype),
-            pltpu.SemaphoreType.DMA((3,)),
+            pltpu.SemaphoreType.DMA((4,)),
         ],
-        dtypes=[bank.dtype, jnp.float32],
+        dtypes=[bank.dtype, jnp.float32, grads.dtype],
     )
     chosen = reduce_row(picked)
     base, part, grads, turned = call(
@@ -404,6 +428,7 @@
         [(mine, rows), pieces, grads.shape, (depth, rows)],
         chosen,
         scale,
+        begin,
         Far(grads),
         scratch=[pltpu.SemaphoreType.DMA((rows_n,))],
         dtypes=[jnp.float32, jnp.float32, grads.dtype, grads.dtype],
@@ -420,7 +445,7 @@
     both = pltpu.VMEM((2 * queries, queries), jnp.float32)
     solved, terms = call(
         functools.partial(first_kernel, width),
-        [(5, queries, queries), (rows, 6 * queries)],
+        [(6, queries, queries), (rows, 6 * queries)],
         back,
         held,
         scratch=[both],

time: 141 us -> 141 us (level)
  no operation moved by 1% of the time
where the time goes in v9:
time: 141 us; the launch traced here: 140 us
  blocking collectives  107 us (76%)
  Pallas kernels  21.1 us (15%)
  waiting for transfers between devices  7.24 us (5%)
  starting transfers between devices  3.54 us (3%)
    all_to_all x8, blocking collectives, swap(): return lax.all_to_all(pieces, axis, 0, 0, tiled=True)  107 us
    pallas_call x11, Pallas kernels, call(): pl.pallas_call(kernel, out_shape=tuple((jax.ShapeDtypeStruct(*shape) for...  21.1 us
    all_to_all x1, waiting for transfers between devices, swap(): return lax.all_to_all(pieces, axis, 0, 0, tiled=True)  7.24 us
    all_to_all x1, starting transfers between devices, swap(): return lax.all_to_all(pieces, axis, 0, 0, tiled=True)  3.54 us
  transfers between devices with their start and end apart: 1, of which 1 were waited for; matrix products, arithmetic and copies ran while one was open for 0% of the time, Pallas kernels for 3%

profile of v9, /device:TPU:1, one launch (start us, length us, event | category | flops | bytes accessed | tf_op | source)
XLA Modules:
  0.0 139.9 jit_solution(1960588176656993764)
XLA Ops:
  0.6 1.2 shard_map.59
  1.8 12.8 %all_to_all.45.parts_ref = bf16[16,8,512]{2,1,0:T(8,128)(2,1)S(1)} all-to-all(bf16[16,8,512]{2,1,0:T(8,128)(2,1)S(1)} %get-tuple-element.15), channel_id=1, replica_groups=mesh['row'=16,'col'=16] {'row'}, dimensions={0} | all-to-all | bytes 262144 | tf_op jit(solution)/shard_map/all_to_all | solution.py:75
  14.7 9.3 %all_to_all.46.chosen_ref = bf16[16,8,512]{2,1,0:T(8,128)(2,1)S(1)} all-to-all(bf16[16,8,512]{2,1,0:T(8,128)(2,1)S(1)} %shard_map.60), channel_id=1, replica_groups=mesh['row'=16,'col'=16] {'row'}, dimensions={0} | all-to-all | bytes 262144 | tf_op jit(solution)/shard_map/all_to_all | solution.py:75
  23.9 5.5 %shard_map.61 = (f32[8,512]{1,0:T(8,128)S(1)}, f32[16,8,512]{2,1,0:T(8,128)S(1)}, bf16[512,8192]{1,0:T(8,128)(2,1)S(1)}, bf16[8192,512]{1,0:T(8,128)(2,1)S(1)}) custom-call(bf16[16,8,512]{2,1,0:T(8,128)(2,1)S(1)} %all_to_all.46.chosen_ref, f32[1,512]{1,0:T(1,128)S(1)} %get-tuple-element.16.scale_ref, bf16[512,512]{1,0:T(8,128)(2,1)S(1)} %get-tuple-element.17.begin_ref, ...), custom_call_target="tpu_custom_call" | custom-call | tf_op jit(solution)/shard_map/pallas_call | solution.py:376
  29.4 10.4 %all_to_all.47.parts_ref = f32[16,8,512]{2,1,0:T(8,128)S(1)} all-to-all(f32[16,8,512]{2,1,0:T(8,128)S(1)} %get-tuple-element.18), channel_id=1, replica_groups=mesh['row'=16,'col'=16] {'row'}, dimensions={0} | all-to-all | bytes 524288 | tf_op jit(solution)/shard_map/all_to_all | solution.py:75
  39.8 10.6 %all_to_all.48.back_ref = f32[16,8,512]{2,1,0:T(8,128)S(1)} all-to-all(f32[16,8,512]{2,1,0:T(8,128)S(1)} %shard_map.62), channel_id=1, replica_groups=mesh['row'=16,'col'=16] {'row'}, dimensions={0} | all-to-all | bytes 524288 | tf_op jit(solution)/shard_map/all_to_all | solution.py:75
  50.5 2.4 %shard_map.63 = (f32[8,1152]{1,0:T(8,128)S(1)}, f32[16,8,512]{2,1,0:T(8,128)S(1)}) custom-call(f32[16,8,512]{2,1,0:T(8,128)S(1)} %all_to_all.48.back_ref, bf16[16,8,512]{2,1,0:T(8,128)(2,1)S(1)} %all_to_all.46.chosen_ref, f32[8,512]{1,0:T(8,128)S(1)} %get-tuple-element.19.base_ref, f32[1,512]{1,0:T(1,128)S(1)} %get-tuple-element.16.scale_ref, ...), custom_call_target="tpu_custom_call" | custom-call | tf_op jit(solution)/shard_map/pallas_call | solution.py:376
  52.9 28.5 %all_to_all.49 = f32[16,8,1152]{2,1,0:T(8,128)S(1)} all-to-all(f32[16,8,1152]{2,1,0:T(8,128)S(1)} %broadcast_in_dim.4), channel_id=1, replica_groups=mesh['row'=16,'col'=16] {'col'}, dimensions={0} | all-to-all | bytes 1179648 | tf_op jit(solution)/shard_map/all_to_all | solution.py:75
  81.4 0.5 shard_map.64
  81.9 14.1 %all_to_all.50.parts_ref = f32[16,8,768]{2,1,0:T(8,128)S(1)} all-to-all(f32[16,8,768]{2,1,0:T(8,128)S(1)} %shard_map.64), channel_id=1, replica_groups=mesh['row'=16,'col'=16] {'row'}, dimensions={0} | all-to-all | bytes 786432 | tf_op jit(solution)/shard_map/all_to_all | solution.py:75
  96.1 12.0 %all_to_all.51.back_ref = f32[16,8,768]{2,1,0:T(8,128)S(1)} all-to-all(f32[16,8,768]{2,1,0:T(8,128)S(1)} %shard_map.65), channel_id=1, replica_groups=mesh['row'=16,'col'=16] {'row'}, dimensions={0} | all-to-all | bytes 786432 | tf_op jit(solution)/shard_map/all_to_all | solution.py:75
  108.1 1.4 shard_map.67
  109.5 9.6 %all_to_all.52.parts_ref = f32[16,8,128]{2,1,0:T(8,128)S(1)} all-to-all(f32[16,8,128]{2,1,0:T(8,128)S(1)} %broadcast_in_dim.5), channel_id=1, replica_groups=mesh['row'=16,'col'=16] {'row'}, dimensions={0} | all-to-all | bytes 131072 | tf_op jit(solution)/shard_map/all_to_all | solution.py:75
  119.1 0.8 shard_map.68
  119.8 3.5 %all-to-all-start.8 = ((f32[16,8,640]{2,1,0:T(8,128)}), f32[16,8,640]{2,1,0:T(8,128)S(1)}, u32[]{:S(2)}, u32[]{:S(2)}) async-start(f32[16,8,640]{2,1,0:T(8,128)} %shard_map.68), calls=%async_computation.8 | async-start | bytes 655360 | tf_op jit(solution)/shard_map/all_to_all | solution.py:75
  123.4 4.3 %shard_map.66 = (f32[6,128,128]{2,1,0:T(8,128)S(1)}, bf16[512,768]{1,0:T(8,128)(2,1)S(1)}) custom-call(f32[16,8,768]{2,1,0:T(8,128)S(1)} %all_to_all.51.back_ref, f32[128,1152]{1,0:T(8,128)S(1)} %bitcast.5), custom_call_target="tpu_custom_call" | custom-call | tf_op jit(solution)/shard_map/pallas_call | solution.py:376
  127.7 7.2 %all-to-all-done.8 = f32[16,8,640]{2,1,0:T(8,128)S(1)} async-done(((f32[16,8,640]{2,1,0:T(8,128)}), f32[16,8,640]{2,1,0:T(8,128)S(1)}, u32[]{:S(2)}, u32[]{:S(2)}) %all-to-all-start.8) | async-done | bytes 327712 | tf_op jit(solution)/shard_map/all_to_all | solution.py:75
  134.9 4.9 %shard_map.69 = (f32[512,128]{1,0:T(8,128)}, f32[512,128]{1,0:T(8,128)}) custom-call(f32[128,1152]{1,0:T(8,128)S(1)} %bitcast.6, f32[6,128,128]{2,1,0:T(8,128)S(1)} %get-tuple-element.24.solved_ref, bf16[512,768]{1,0:T(8,128)(2,1)S(1)} %get-tuple-element.25.terms_ref, f32[128,640]{1,0:T(8,128)S(1)} %bitcast.7), custom_call_target="tpu_custom_call" | custom-call | tf_op jit(solution)/shard_map/pallas_call | solution.py:376
  (5 shorter events, 0.2 us)
Async XLA Ops:
  119.8 15.1 %all-to-all-start.8 = ((f32[16,8,640]{2,1,0:T(8,128)}), f32[16,8,640]{2,1,0:T(8,128)S(1)}, u32[]{:S(2)}, u32[]{:S(2)}) async-start(f32[16,8,640]{2,1,0:T(8,128)} %shard_map.68), calls=%async_computation.8 | async-start | bytes 655360 | tf_op jit(solution)/shard_map/all_to_all | solution.py:75

commit v10 on v9

--- a/solution.py
+++ b/solution.py
@@ -207,18 +207,20 @@
     for k in range(parts):
         block = (slice(None), pl.ds(k * width, width))
         copies.append(pltpu.make_async_copy(grads_hbm.at[block], grads_ref.at[block], sems.at[k]))
-    for copy in copies[1:] + copies[:1]:
+    ready = begin_ref.shape[1] // width
+    for copy in copies[ready:] + copies[:ready]:
         copy.start()
     total = jnp.zeros(base_ref.shape, jnp.float32)
     for k in range(parts):
-        if k == 0:
-            turned = begin_ref[...].T
+        if k < ready:
+            turned = begin_ref[:, k * width : (k + 1) * width].T
         else:
             copies[k].wait()
             turned = grads_ref[:, k * width : (k + 1) * width].T
         turned_ref[k * width : (k + 1) * width] = turned
         total += bf16_dot(chosen_ref[k], turned, 0)
-    copies[0].wait()
+    for copy in copies[:ready]:
+        copy.wait()
     scale = scale_ref[...]
     base = scale * total
     base_ref[...] = base
@@ -409,7 +411,7 @@
     seeds = seeds.reshape(-1, lanes)
     picked, scale, begin = call(
         pick_kernel,
-        [pieces, (1, rows), (rows, pieces[2])],
+        [pieces, (1, rows), (rows, 4 * pieces[2])],
         Far(query_ids),
         Far(seeds),
         Far(bank),

time: 141 us -> 141 us (level)
  no operation moved by 1% of the time
where the time goes in v10:
time: 141 us; the launch traced here: 140 us
  blocking collectives  107 us (76%)
  Pallas kernels  21.5 us (15%)
  waiting for transfers between devices  7.23 us (5%)
  starting transfers between devices  3.54 us (3%)
    all_to_all x8, blocking collectives, swap(): return lax.all_to_all(pieces, axis, 0, 0, tiled=True)  107 us
    pallas_call x11, Pallas kernels, call(): pl.pallas_call(kernel, out_shape=tuple((jax.ShapeDtypeStruct(*shape) for...  21.5 us
    all_to_all x1, waiting for transfers between devices, swap(): return lax.all_to_all(pieces, axis, 0, 0, tiled=True)  7.23 us
    all_to_all x1, starting transfers between devices, swap(): return lax.all_to_all(pieces, axis, 0, 0, tiled=True)  3.54 us
  transfers between devices with their start and end apart: 1, of which 1 were waited for; matrix products, arithmetic and copies ran while one was open for 0% of the time, Pallas kernels for 3%

profile of v10, /device:TPU:1, one launch (start us, length us, event | category | flops | bytes accessed | tf_op | source)
XLA Modules:
  0.0 140.3 jit_solution(17055301508770384034)
XLA Ops:
  0.6 1.7 %shard_map.59 = (bf16[16,8,512]{2,1,0:T(8,128)(2,1)S(1)}, f32[1,512]{1,0:T(1,128)S(1)}, bf16[512,2048]{1,0:T(8,128)(2,1)S(1)}) custom-call(s32[128]{0:T(128)} %ids_hbm.1, s32[64,128]{1,0:T(8,128)} %bitcast.8, bf16[16,8192]{1,0:T(8,128)(2,1)} %bank_hbm.1, bf16[512,8192]{1,0:T(8,128)(2,1)} %grads_hbm.3), custom_call_target="tpu_custom_call" | custom-call | tf_op jit(solution)/shard_map/pallas_call | solution.py:378
  2.4 12.8 %all_to_all.45.parts_ref = bf16[16,8,512]{2,1,0:T(8,128)(2,1)S(1)} all-to-all(bf16[16,8,512]{2,1,0:T(8,128)(2,1)S(1)} %get-tuple-element.15), channel_id=1, replica_groups=mesh['row'=16,'col'=16] {'row'}, dimensions={0} | all-to-all | bytes 262144 | tf_op jit(solution)/shard_map/all_to_all | solution.py:75
  15.2 9.3 %all_to_all.46.chosen_ref = bf16[16,8,512]{2,1,0:T(8,128)(2,1)S(1)} all-to-all(bf16[16,8,512]{2,1,0:T(8,128)(2,1)S(1)} %shard_map.60), channel_id=1, replica_groups=mesh['row'=16,'col'=16] {'row'}, dimensions={0} | all-to-all | bytes 262144 | tf_op jit(solution)/shard_map/all_to_all | solution.py:75
  24.5 5.4 %shard_map.61 = (f32[8,512]{1,0:T(8,128)S(1)}, f32[16,8,512]{2,1,0:T(8,128)S(1)}, bf16[512,8192]{1,0:T(8,128)(2,1)S(1)}, bf16[8192,512]{1,0:T(8,128)(2,1)S(1)}) custom-call(bf16[16,8,512]{2,1,0:T(8,128)(2,1)S(1)} %all_to_all.46.chosen_ref, f32[1,512]{1,0:T(1,128)S(1)} %get-tuple-element.16.scale_ref, bf16[512,2048]{1,0:T(8,128)(2,1)S(1)} %get-tuple-element.17.begin_ref, ...), custom_call_target="tpu_custom_call" | custom-call | tf_op jit(solution)/shard_map/pallas_call | solution.py:378
  29.8 10.4 %all_to_all.47.parts_ref = f32[16,8,512]{2,1,0:T(8,128)S(1)} all-to-all(f32[16,8,512]{2,1,0:T(8,128)S(1)} %get-tuple-element.18), channel_id=1, replica_groups=mesh['row'=16,'col'=16] {'row'}, dimensions={0} | all-to-all | bytes 524288 | tf_op jit(solution)/shard_map/all_to_all | solution.py:75
  40.2 10.6 %all_to_all.48.back_ref = f32[16,8,512]{2,1,0:T(8,128)S(1)} all-to-all(f32[16,8,512]{2,1,0:T(8,128)S(1)} %shard_map.62), channel_id=1, replica_groups=mesh['row'=16,'col'=16] {'row'}, dimensions={0} | all-to-all | bytes 524288 | tf_op jit(solution)/shard_map/all_to_all | solution.py:75
  50.9 2.4 %shard_map.63 = (f32[8,1152]{1,0:T(8,128)S(1)}, f32[16,8,512]{2,1,0:T(8,128)S(1)}) custom-call(f32[16,8,512]{2,1,0:T(8,128)S(1)} %all_to_all.48.back_ref, bf16[16,8,512]{2,1,0:T(8,128)(2,1)S(1)} %all_to_all.46.chosen_ref, f32[8,512]{1,0:T(8,128)S(1)} %get-tuple-element.19.base_ref, f32[1,512]{1,0:T(1,128)S(1)} %get-tuple-element.16.scale_ref, ...), custom_call_target="tpu_custom_call" | custom-call | tf_op jit(solution)/shard_map/pallas_call | solution.py:378
  53.3 28.5 %all_to_all.49 = f32[16,8,1152]{2,1,0:T(8,128)S(1)} all-to-all(f32[16,8,1152]{2,1,0:T(8,128)S(1)} %broadcast_in_dim.4), channel_id=1, replica_groups=mesh['row'=16,'col'=16] {'col'}, dimensions={0} | all-to-all | bytes 1179648 | tf_op jit(solution)/shard_map/all_to_all | solution.py:75
  81.8 0.5 shard_map.64
  82.3 14.1 %all_to_all.50.parts_ref = f32[16,8,768]{2,1,0:T(8,128)S(1)} all-to-all(f32[16,8,768]{2,1,0:T(8,128)S(1)} %shard_map.64), channel_id=1, replica_groups=mesh['row'=16,'col'=16] {'row'}, dimensions={0} | all-to-all | bytes 786432 | tf_op jit(solution)/shard_map/all_to_all | solution.py:75
  96.5 12.0 %all_to_all.51.back_ref = f32[16,8,768]{2,1,0:T(8,128)S(1)} all-to-all(f32[16,8,768]{2,1,0:T(8,128)S(1)} %shard_map.65), channel_id=1, replica_groups=mesh['row'=16,'col'=16] {'row'}, dimensions={0} | all-to-all | bytes 786432 | tf_op jit(solution)/shard_map/all_to_all | solution.py:75
  108.5 1.4 shard_map.67
  109.9 9.6 %all_to_all.52.parts_ref = f32[16,8,128]{2,1,0:T(8,128)S(1)} all-to-all(f32[16,8,128]{2,1,0:T(8,128)S(1)} %broadcast_in_dim.5), channel_id=1, replica_groups=mesh['row'=16,'col'=16] {'row'}, dimensions={0} | all-to-all | bytes 131072 | tf_op jit(solution)/shard_map/all_to_all | solution.py:75
  119.5 0.8 shard_map.68
  120.2 3.5 %all-to-all-start.8 = ((f32[16,8,640]{2,1,0:T(8,128)}), f32[16,8,640]{2,1,0:T(8,128)S(1)}, u32[]{:S(2)}, u32[]{:S(2)}) async-start(f32[16,8,640]{2,1,0:T(8,128)} %shard_map.68), calls=%async_computation.8 | async-start | bytes 655360 | tf_op jit(solution)/shard_map/all_to_all | solution.py:75
  123.8 4.3 %shard_map.66 = (f32[6,128,128]{2,1,0:T(8,128)S(1)}, bf16[512,768]{1,0:T(8,128)(2,1)S(1)}) custom-call(f32[16,8,768]{2,1,0:T(8,128)S(1)} %all_to_all.51.back_ref, f32[128,1152]{1,0:T(8,128)S(1)} %bitcast.5), custom_call_target="tpu_custom_call" | custom-call | tf_op jit(solution)/shard_map/pallas_call | solution.py:378
  128.1 7.2 %all-to-all-done.8 = f32[16,8,640]{2,1,0:T(8,128)S(1)} async-done(((f32[16,8,640]{2,1,0:T(8,128)}), f32[16,8,640]{2,1,0:T(8,128)S(1)}, u32[]{:S(2)}, u32[]{:S(2)}) %all-to-all-start.8) | async-done | bytes 327712 | tf_op jit(solution)/shard_map/all_to_all | solution.py:75
  135.3 4.9 %shard_map.69 = (f32[512,128]{1,0:T(8,128)}, f32[512,128]{1,0:T(8,128)}) custom-call(f32[128,1152]{1,0:T(8,128)S(1)} %bitcast.6, f32[6,128,128]{2,1,0:T(8,128)S(1)} %get-tuple-element.24.solved_ref, bf16[512,768]{1,0:T(8,128)(2,1)S(1)} %get-tuple-element.25.terms_ref, f32[128,640]{1,0:T(8,128)S(1)} %bitcast.7), custom_call_target="tpu_custom_call" | custom-call | tf_op jit(solution)/shard_map/pallas_call | solution.py:378
  (5 shorter events, 0.2 us)
Async XLA Ops:
  120.2 15.1 %all-to-all-start.8 = ((f32[16,8,640]{2,1,0:T(8,128)}), f32[16,8,640]{2,1,0:T(8,128)S(1)}, u32[]{:S(2)}, u32[]{:S(2)}) async-start(f32[16,8,640]{2,1,0:T(8,128)} %shard_map.68), calls=%async_computation.8 | async-start | bytes 655360 | tf_op jit(solution)/shard_map/all_to_all | solution.py:75
